TPU v7x, 256 devices: a whole 4x4x8 slice. The times are simulated.
256 devices in a mesh: group: 2 (over x_hi), seq: 8 (over y, core), mp: 16 (over x_lo, z).
Axes of the slice: x: 4 (x_hi: 2, x_lo: 2; x = x_hi * 2 + x_lo), y: 4, z: 8, core: 2. Of those that a mesh axis runs over, the one named last changes fastest.
Arguments:
- image_tokens: bfloat16 [1024, 1280], P(('group', 'seq')), may hold values from -6 to 6
- ln_gain: float32 [1280], replicated, may hold values from 0.25 to 1.75
- ln_bias: float32 [1280], replicated, may hold values from -3 to 3
- mlp_in: bfloat16 [1280, 5120], P(None, 'mp'), may hold values from -0.15625 to 0.15625
- mlp_out: bfloat16 [5120, 1280], P('mp'), may hold values from -0.078125 to 0.078125
- key_proj: bfloat16 [1280, 1024], P(None, 'mp'), may hold values from -0.15625 to 0.15625
- value_proj: bfloat16 [1280, 1024], P(None, 'mp'), may hold values from -0.15625 to 0.15625
- text_tokens: bfloat16 [2048, 4096], P(('group', 'seq')), may hold values from -6 to 6
- text_gain: float32 [4096], replicated, may hold values from 0.25 to 1.75
- query_proj: bfloat16 [4096, 4096], P('seq', 'mp'), may hold values from -0.09375 to 0.09375
- output_proj: bfloat16 [4096, 4096], P('seq', 'mp'), may hold values from -0.09375 to 0.09375
- attn_gate: float32 [1], replicated, may hold values from 0.4 to 1.2
- doc_image: int32 [16], P(('group', 'seq')), may hold values from -1 to 1
- out_cotangent: bfloat16 [2048, 4096], P(('group', 'seq')), may hold values from -6 to 6
Outputs:
- text_out: bfloat16 [2048, 4096], P(('group', 'seq'), 'mp')
- image_grad: float32 [1024, 1280], P(('group', 'seq'))
Inputs may be any that keep to these rules, and one draw needn't show every extreme that they name: `doc_image`: entry b names the image that text tokens b * 128 to (b + 1) * 128 - 1 read; -1 means the block reads no image.
All inputs are finite; a program needn't handle non-finite values.
Results may differ from a plain program's by a relative error of at most 0.014.
Values may be sent and summed in bfloat16 or wider, within the bound.
No kernel may reach another device: no remote copies, remote signals or barrier semaphores. Data moves between devices by JAX's collectives and lax.ppermute only.
A program may use at most 64 MiB of HBM per device.

v0:
```python
import jax
import jax.numpy as jnp
from jax import lax
from jax.experimental import pallas as pl
from jax.experimental.pallas import tpu as pltpu
from jax.sharding import PartitionSpec as P


HT = 128
EPS_VISION = 1e-06
EPS_TEXT = 1e-05
GELU_COEF = 0.7978845608028654
CUBIC_COEF = 0.044715

NEAR = (1, 8, 9)
FAR = (4, 2, 6)
NEAR_SETS = [[b, b + 1, b + 8, b + 9] for b in (0, 2, 4, 6)]
ALONG_Y = [[0, 2, 4, 6], [1, 3, 5, 7]]


F32 = jnp.float32
BF16 = jnp.bfloat16


def exchanged(x, axis, groups):
    return lax.all_to_all(x, axis, 0, 0, tiled=True, axis_index_groups=groups)


def swapped(x, axis, mask):
    return lax.ppermute(x, axis, [(i, i ^ mask) for i in range(lax.axis_size(axis))])


def gelu_parts(pre_act):
    cube_term = pre_act * pre_act * pre_act
    tangent = jnp.tanh(GELU_COEF * (pre_act + CUBIC_COEF * cube_term))
    gelu_value = 0.5 * pre_act * (1.0 + tangent)
    gelu_slope = 0.5 * (1.0 + tangent) + 0.5 * pre_act * (1.0 - tangent * tangent) * GELU_COEF * (
        1.0 + 3.0 * CUBIC_COEF * pre_act * pre_act
    )
    return (gelu_value, gelu_slope)


def layer_norm(image_tokens, ln_gain, ln_bias):
    image_float = image_tokens.astype(F32)
    centred = image_float - jnp.mean(image_float, axis=1, keepdims=True)
    inv_scale = lax.rsqrt(jnp.mean(centred * centred, axis=1, keepdims=True) + EPS_VISION)
    normed_hat = centred * inv_scale
    normed = (normed_hat * ln_gain + ln_bias).astype(BF16)
    return (image_float, normed_hat, inv_scale, normed)


def norm_backward(d_normed, normed_hat, inv_scale, ln_gain):
    scaled = d_normed * ln_gain
    first_mean = jnp.mean(scaled, axis=1, keepdims=True)
    second_mean = jnp.mean(scaled * normed_hat, axis=1, keepdims=True)
    return inv_scale * (scaled - first_mean - normed_hat * second_mean)


def contract_last(left, right):
    return lax.dot_general(left, right, (((1,), (1,)), ((), ())), preferred_element_type=F32)


def reduced_chunk(term):
    near = [swapped(term[k].astype(BF16), "mp", NEAR[k - 1]).astype(F32) for k in (1, 2, 3)]
    part = ((term[0] + near[0]) + (near[1] + near[2])).astype(BF16)
    far = [swapped(part, "mp", mask).astype(F32) for mask in FAR]
    return (part.astype(F32) + far[1]) + (far[0] + far[2])


def gathered_chunks(chunk):
    return jnp.stack([chunk] + [swapped(chunk, "mp", mask) for mask in NEAR])


def spread_kernel(first, second, out, held, sems):
    rows = first.shape[0]
    copies = [
        pltpu.make_async_copy(ref, held.at[pl.ds(i * rows, rows)], sems.at[i])
        for i, ref in enumerate((first, second))
    ]
    for copy in copies:
        copy.start()
    for copy in copies:
        copy.wait()
    copies = [pltpu.make_async_copy(held, out.at[i], sems.at[2 + i]) for i in range(out.shape[0])]
    for copy in copies:
        copy.start()
    for copy in copies:
        copy.wait()


def text_kernel(doc, gate, gain, own, other, tokens_in, cot_in, q_out, d_out, tokens, cot, normed, d_proj, sems):
    copies = [
        pltpu.make_async_copy(tokens_in, tokens, sems.at[0]),
        pltpu.make_async_copy(cot_in, cot, sems.at[1]),
    ]
    for copy in copies:
        copy.start()
    core = lax.axis_index("seq") & 1
    copies[0].wait()
    x = tokens[...].astype(F32)
    scale = lax.rsqrt(jnp.mean(x * x, axis=1, keepdims=True) + EPS_TEXT)
    normed[...] = (x * scale * gain[...]).astype(BF16)
    copies[1].wait()
    has_image = jnp.where(doc[0] >= 0, 1.0, 0.0)
    d_proj[...] = (jnp.tanh(gate[...]) * has_image * cot[...].astype(F32)).astype(BF16)
    rows, depth = tokens.shape[0], own.shape[1] // 2
    total_q = jnp.zeros((rows, q_out.shape[1]), F32)
    total_d = jnp.zeros((rows, d_out.shape[1]), F32)
    for y in range(own.shape[0]):
        for ref, side in ((own, core), (other, 1 - core)):
            cols = pl.ds(pl.multiple_of((2 * y + side) * depth, depth), depth)
            total_q += jnp.dot(normed[:, cols], ref[y, :depth], preferred_element_type=F32)
            total_d += jnp.dot(d_proj[:, cols], ref[y, depth:], preferred_element_type=F32)
    q_out[...] = total_q.astype(BF16)
    d_out[...] = total_d.astype(BF16)


def attend_kernel(doc, q, d, own, other, att_out, g_own, g_other):
    r = jnp.maximum(doc[0], 0) ^ lax.axis_index("group")
    peers, _, image_rows, _ = own.shape
    blocks = [ref[k, r] for ref in (own, other) for k in range(peers)]
    keys = jnp.concatenate([b[:, :HT] for b in blocks], axis=0)
    values = jnp.concatenate([b[:, HT:] for b in blocks], axis=0)
    head_scale = HT ** (-0.5)
    key_grads = jnp.zeros(keys.shape, F32)
    value_grads = jnp.zeros(keys.shape, F32)
    odd = (lax.axis_index("mp") & 1) == 1

    def turned(x):
        return jnp.where(odd, jnp.concatenate([x[:, HT // 2 :], x[:, : HT // 2]], axis=1), x)

    for h in range(q.shape[1] // HT):
        cols = slice(h * HT, (h + 1) * HT)
        qh, dh = turned(q[:, cols]), turned(d[:, cols])
        scores = contract_last(keys, qh) * head_scale
        expo = jnp.exp(scores - jnp.max(scores, axis=0, keepdims=True))
        soft = expo / jnp.sum(expo, axis=0, keepdims=True)
        half = soft.astype(BF16)
        att = lax.dot_general(half, values, (((0,), (0,)), ((), ())), preferred_element_type=F32)
        att_out[:, cols] = turned(att).astype(BF16)
        d_probs = contract_last(values, dh)
        delta = jnp.sum(half.astype(F32) * d_probs, axis=0, keepdims=True)
        d_scores = (soft * (d_probs - delta)).astype(BF16)
        value_grads += jnp.dot(half, dh, preferred_element_type=F32)
        key_grads += jnp.dot(d_scores, qh, preferred_element_type=F32)
    grads = jnp.concatenate([key_grads * head_scale, value_grads], axis=1).astype(BF16)
    nothing = jnp.zeros((image_rows, 2 * HT), BF16)
    for i, ref in enumerate((g_own, g_other)):
        for k in range(peers):
            at = (i * peers + k) * image_rows
            ref[r, k] = grads[at : at + image_rows]
            ref[1 - r, k] = nothing


def term_kernel(att, own, other, out):
    core, m = lax.axis_index("seq") & 1, lax.axis_index("mp")
    depth, width = own.shape[1] // 2, out.shape[2]
    for y in range(own.shape[0]):
        for ref, side in ((own, core), (other, 1 - core)):
            term = contract_last(att[...], ref[y, depth:]).astype(BF16)
            for half in range(depth // width):
                to = (2 * y + side) * (depth // width) + half
                near = (to & 1) | ((to >> 3) << 1)
                out[near * 4 + (((to ^ m) >> 1) & 3)] = term[:, half * width : (half + 1) * width]


def sum_kernel(arrived, kept, sent):
    for k in range(arrived.shape[1]):
        parts = [arrived[i, k].astype(F32) for i in range(arrived.shape[0])]
        total = (parts[0] + parts[1]) + (parts[2] + parts[3])
        if k in (1, 2):
            sent[k - 1] = total.astype(BF16)
        else:
            kept[k // 2] = total


VMEM = pl.BlockSpec(memory_space=pltpu.VMEM)
SMEM = pl.BlockSpec(memory_space=pltpu.SMEM)
HBM = pl.BlockSpec(memory_space=pltpu.HBM)
SMALL_VMEM = pltpu.CompilerParams(vmem_limit_bytes=16 * 1024 * 1024)


def shards(
    image_tokens,
    ln_gain,
    ln_bias,
    mlp_in,
    mlp_out,
    key_proj,
    value_proj,
    text_tokens,
    text_gain,
    query_proj,
    output_proj,
    attn_gate,
    doc_image,
    out_cotangent,
):
    m = lax.axis_index("mp")
    image_rows, vision_width = image_tokens.shape
    text_rows, text_width = text_tokens.shape
    out_width = text_width // lax.axis_size("mp")
    near_index = (m & 1) | ((m >> 3) << 1)
    chunk_rows = image_rows // 4

    depth, head_cols = query_proj.shape
    spread = pl.pallas_call(
        spread_kernel,
        out_shape=jax.ShapeDtypeStruct((4, 2 * depth, head_cols), BF16),
        in_specs=[HBM] * 2,
        out_specs=HBM,
        scratch_shapes=[pltpu.VMEM((2 * depth, head_cols), BF16), pltpu.SemaphoreType.DMA((6,))],
        compiler_params=SMALL_VMEM,
        name="spread",
    )(query_proj, output_proj)
    along = exchanged(spread, "seq", ALONG_Y)
    weights = [along, swapped(along, "seq", 1)]

    lines = image_tokens.reshape(4, chunk_rows, vision_width)
    ordered = jnp.concatenate(
        [lax.dynamic_slice_in_dim(lines, near_index ^ k, 1, 0) for k in range(4)], axis=0
    ).reshape(image_rows, vision_width)
    image_float, normed_hat, inv_scale, normed = layer_norm(ordered, ln_gain, ln_bias)
    pre_act = jnp.dot(normed, mlp_in, preferred_element_type=F32)
    gelu_value, gelu_slope = gelu_parts(pre_act)
    mlp_term = jnp.dot(gelu_value.astype(BF16), mlp_out, preferred_element_type=F32)
    mlp_chunk = reduced_chunk(mlp_term.reshape(4, chunk_rows, vision_width))
    state_chunk = (image_float[:chunk_rows] + mlp_chunk).astype(BF16)
    image_state = gathered_chunks(state_chunk).reshape(image_rows, vision_width)

    partner_kv = swapped(jnp.stack([key_proj, value_proj]), "mp", 1)
    kv_cols = jnp.concatenate([key_proj, partner_kv[0], value_proj, partner_kv[1]], axis=1)
    local_kv = jnp.dot(image_state, kv_cols, preferred_element_type=F32).astype(BF16)
    both = jnp.stack([local_kv, swapped(local_kv, "group", 1)])
    own_core = jnp.stack([both] + [swapped(both, "seq", 2 * k) for k in (1, 2, 3)])
    other_core = swapped(own_core, "seq", 1)

    small = jax.ShapeDtypeStruct((text_rows, head_cols), BF16)
    wide = pltpu.VMEM((text_rows, text_width), BF16)
    queries, d_attended = pl.pallas_call(
        text_kernel,
        out_shape=(small, small),
        in_specs=[SMEM] + [VMEM] * 4 + [HBM] * 2,
        out_specs=(VMEM, VMEM),
        scratch_shapes=[wide] * 4 + [pltpu.SemaphoreType.DMA((2,))],
        compiler_params=SMALL_VMEM,
        name="text_projections",
    )(
        doc_image,
        attn_gate.reshape(1, 1),
        text_gain.reshape(1, text_width),
        *weights,
        *[pltpu.with_memory_space_constraint(x, pltpu.HBM) for x in (text_tokens, out_cotangent)],
    )

    grid = jax.ShapeDtypeStruct((2, 4, image_rows, 2 * HT), BF16)
    attended, grads_own, grads_other = pl.pallas_call(
        attend_kernel,
        out_shape=(small, grid, grid),
        in_specs=[SMEM] + [VMEM] * 4,
        out_specs=(VMEM, VMEM, VMEM),
        compiler_params=SMALL_VMEM,
        name="attention",
    )(doc_image, queries, d_attended, own_core, other_core)

    summed = grads_own.astype(F32) + swapped(grads_other, "seq", 1).astype(F32)
    summed = summed[0] + swapped(summed[1].astype(BF16), "group", 1).astype(F32)
    along_y = [swapped(summed[k].astype(BF16), "seq", 2 * k).astype(F32) for k in (1, 2, 3)]
    kv_grads = (summed[0] + along_y[0]) + (along_y[1] + along_y[2])
    state_term = contract_last(kv_grads.astype(BF16), kv_cols)
    state_chunk_grad = reduced_chunk(state_term.reshape(4, chunk_rows, vision_width))
    state_half = gathered_chunks(state_chunk_grad.astype(BF16)).reshape(image_rows, vision_width)
    d_hidden = contract_last(state_half, mlp_out)
    d_pre = (d_hidden * gelu_slope).astype(BF16)
    normed_term = contract_last(d_pre, mlp_in)
    d_normed = reduced_chunk(normed_term.reshape(4, chunk_rows, vision_width))
    grad_chunk = state_chunk_grad + norm_backward(
        d_normed, normed_hat[:chunk_rows], inv_scale[:chunk_rows], ln_gain
    )
    grads = gathered_chunks(grad_chunk.astype(BF16))
    image_grad = jnp.concatenate(
        [lax.dynamic_slice_in_dim(grads, near_index ^ k, 1, 0) for k in range(4)], axis=0
    ).reshape(image_rows, vision_width).astype(F32)

    terms = pl.pallas_call(
        term_kernel,
        out_shape=jax.ShapeDtypeStruct((16, text_rows, out_width), BF16),
        in_specs=[VMEM] * 3,
        out_specs=VMEM,
        compiler_params=SMALL_VMEM,
        name="text_terms",
    )(attended, *weights)
    terms = terms.reshape(4, 4, text_rows, out_width)
    kept, sent = pl.pallas_call(
        sum_kernel,
        out_shape=(
            jax.ShapeDtypeStruct((2, text_rows, out_width), F32),
            jax.ShapeDtypeStruct((2, text_rows, out_width), BF16),
        ),
        in_specs=[VMEM],
        out_specs=(VMEM, VMEM),
        compiler_params=SMALL_VMEM,
        name="near_sum",
    )(exchanged(terms, "mp", NEAR_SETS))
    passed = swapped(sent, "mp", 2).astype(F32)
    last = swapped((kept[1] + passed[1]).astype(BF16), "mp", 6).astype(F32)
    text_share = kept[0] + passed[0] + last
    text_slice = lax.dynamic_slice_in_dim(text_tokens, m * out_width, out_width, 1).astype(F32)
    has_image = jnp.where(doc_image[0] >= 0, 1.0, 0.0)
    text_out = (text_slice + jnp.tanh(attn_gate[0]) * has_image * text_share).astype(BF16)
    return (text_out, image_grad)


def solution(mesh):
    return jax.shard_map(
        shards,
        mesh=mesh,
        in_specs=(
            P(("group", "seq"), None),
            P(),
            P(),
            P(None, "mp"),
            P("mp", None),
            P(None, "mp"),
            P(None, "mp"),
            P(("group", "seq"), None),
            P(),
            P("seq", "mp"),
            P("seq", "mp"),
            P(),
            P(("group", "seq")),
            P(("group", "seq"), None),
        ),
        out_specs=(P(("group", "seq"), "mp"), P(("group", "seq"), None)),
        check_vma=False,
    )
```

profile of v0, /device:TPU:32, one launch (start us, length us, event | category | flops | bytes accessed | tf_op | source)
XLA Modules:
  0.0 168.2 jit_solution(17100460118534911524)
XLA Ops:
  4.2 4.6 %all-to-all-start = ((bf16[4,1024,256]{2,1,0:T(8,128)(2,1)}), bf16[4,1024,256]{2,1,0:T(8,128)(2,1)S(1)}, u32[]{:S(2)}, u32[]{:S(2)}) async-start(bf16[4,1024,256]{2,1,0:T(8,128)(2,1)} %copy-done.1), calls=%async_computation | async-start | bytes 4194304 | tf_op jit(solution)/shard_map/all_to_all | solution.py:26
  19.6 3.4 %collective-permute-start.4 = (bf16[16,1280]{1,0:T(8,128)(2,1)S(1)}, bf16[16,1280]{1,0:T(8,128)(2,1)S(1)}, u32[]{:S(2)}, u32[]{:S(2)}) collective-permute-start(bf16[16,1280]{1,0:T(8,128)(2,1)S(1)} %fusion.35), channel_id=1, source_target_pairs={{0,2},{1,3},{2,0},{3,1},{4,6},{5,7},{6,4},{7,5},{8,10},{9,11},{10,... | collective-permute-start | bytes 122888 | tf_op jit(solution)/shard_map/ppermute | solution.py:30
  23.0 5.4 %collective-permute-start.5 = (bf16[16,1280]{1,0:T(8,128)(2,1)S(1)}, bf16[16,1280]{1,0:T(8,128)(2,1)S(1)}, u32[]{:S(2)}, u32[]{:S(2)}) collective-permute-start(bf16[16,1280]{1,0:T(8,128)(2,1)S(1)} %fusion.35), channel_id=1, source_target_pairs={{0,4},{1,5},{2,6},{3,7},{4,0},{5,1},{6,2},{7,3},{8,12},{9,13},{10,... | collective-permute-start | bytes 122888 | tf_op jit(solution)/shard_map/ppermute | solution.py:30
  28.4 6.7 %all-to-all-done.own = bf16[4,1024,256]{2,1,0:T(8,128)(2,1)S(1)} async-done(((bf16[4,1024,256]{2,1,0:T(8,128)(2,1)}), bf16[4,1024,256]{2,1,0:T(8,128)(2,1)S(1)}, u32[]{:S(2)}, u32[]{:S(2)}) %all-to-all-start) | async-done | bytes 2097184 | tf_op jit(solution)/shard_map/all_to_all | solution.py:26
  37.3 2.0 %collective-permute-start.7 = (bf16[16,1280]{1,0:T(8,128)(2,1)S(1)}, bf16[16,1280]{1,0:T(8,128)(2,1)S(1)}, u32[]{:S(2)}, u32[]{:S(2)}) collective-permute-start(bf16[16,1280]{1,0:T(8,128)(2,1)S(1)} %fusion.37), channel_id=1, source_target_pairs={{0,1},{1,0},{2,3},{3,2},{4,5},{5,4},{6,7},{7,6},{8,9},{9,8},{10,11... | collective-permute-start | bytes 122888 | tf_op jit(solution)/shard_map/ppermute | solution.py:30
  40.9 6.8 %collective-permute-done.7 = bf16[16,1280]{1,0:T(8,128)(2,1)S(1)} collective-permute-done((bf16[16,1280]{1,0:T(8,128)(2,1)S(1)}, bf16[16,1280]{1,0:T(8,128)(2,1)S(1)}, u32[]{:S(2)}, u32[]{:S(2)}) %collective-permute-start.7) | collective-permute-done | bytes 40992 | tf_op jit(solution)/shard_map/ppermute | solution.py:30
  50.4 2.8 %collective-permute-start.11 = (bf16[64,256]{1,0:T(8,128)(2,1)S(1)}, bf16[64,256]{1,0:T(8,128)(2,1)S(1)}, u32[]{:S(2)}, u32[]{:S(2)}) collective-permute-start(bf16[64,256]{1,0:T(8,128)(2,1)S(1)} %convolution_convert_fusion), channel_id=1, source_target_pairs={{0,128},{128,0},{1,129},{129,1},{2,130},{130,2},{3,131},{131,3},{4... | collective-permute-start | bytes 98312 | tf_op jit(solution)/shard_map/ppermute | solution.py:30
  53.3 2.7 %collective-permute-done.11 = bf16[64,256]{1,0:T(8,128)(2,1)S(1)} collective-permute-done((bf16[64,256]{1,0:T(8,128)(2,1)S(1)}, bf16[64,256]{1,0:T(8,128)(2,1)S(1)}, u32[]{:S(2)}, u32[]{:S(2)}) %collective-permute-start.11) | collective-permute-done | bytes 32800 | tf_op jit(solution)/shard_map/ppermute | solution.py:30
  56.6 2.1 %collective-permute-start.13 = (bf16[2,64,256]{2,1,0:T(8,128)(2,1)S(1)}, bf16[2,64,256]{2,1,0:T(8,128)(2,1)S(1)}, u32[]{:S(2)}, u32[]{:S(2)}) collective-permute-start(bf16[2,64,256]{2,1,0:T(8,128)(2,1)S(1)} %get-tuple-element.44), channel_id=1, source_target_pairs={{0,64},{16,80},{32,96},{48,112},{64,0},{80,16},{96,32},{112,48},{1... | collective-permute-start | bytes 196616 | tf_op jit(solution)/shard_map/ppermute | solution.py:30
  58.7 2.1 %collective-permute-start.14 = (bf16[2,64,256]{2,1,0:T(8,128)(2,1)S(1)}, bf16[2,64,256]{2,1,0:T(8,128)(2,1)S(1)}, u32[]{:S(2)}, u32[]{:S(2)}) collective-permute-start(bf16[2,64,256]{2,1,0:T(8,128)(2,1)S(1)} %get-tuple-element.44), channel_id=1, source_target_pairs={{0,96},{16,112},{32,64},{48,80},{64,32},{80,48},{96,0},{112,16},{1... | collective-permute-start | bytes 196616 | tf_op jit(solution)/shard_map/ppermute | solution.py:30
  65.8 3.4 %text_projections.1 = (bf16[128,256]{1,0:T(8,128)(2,1)S(1)}, bf16[128,256]{1,0:T(8,128)(2,1)S(1)}) custom-call(s32[1]{0:T(128)S(6)} %copy.17.doc, f32[1,1]{1,0:T(1,128)} %bitcast.89.gate, f32[1,4096]{1,0:T(1,128)S(1)} %bitcast.91, bf16[4,1024,256]{2,1,0:T(8,128)(2,1)S(1)} %all-to-all-done.own, bf16[4,1024,256]{2,1,0:T(8,128)(2,1)S(1)} %collective-permute-done.other, ...), custom_call_target="tpu_custom_call" | custom-call | tf_op jit(solution)/shard_map/text_projections/pallas_call | solution.py:240
  72.2 2.8 %collective-permute-start.19 = (bf16[4,64,256]{2,1,0:T(8,128)(2,1)S(1)}, bf16[4,64,256]{2,1,0:T(8,128)(2,1)S(1)}, u32[]{:S(2)}, u32[]{:S(2)}) collective-permute-start(bf16[4,64,256]{2,1,0:T(8,128)(2,1)S(1)} %fusion.7), channel_id=1, source_target_pairs={{0,128},{128,0},{1,129},{129,1},{2,130},{130,2},{3,131},{131,3},{4... | collective-permute-start | bytes 393224 | tf_op jit(solution)/shard_map/ppermute | solution.py:30
  75.1 4.5 %collective-permute-done.19 = bf16[4,64,256]{2,1,0:T(8,128)(2,1)S(1)} collective-permute-done((bf16[4,64,256]{2,1,0:T(8,128)(2,1)S(1)}, bf16[4,64,256]{2,1,0:T(8,128)(2,1)S(1)}, u32[]{:S(2)}, u32[]{:S(2)}) %collective-permute-start.19) | collective-permute-done | bytes 131104 | tf_op jit(solution)/shard_map/ppermute | solution.py:30
  79.8 3.5 %collective-permute-start.21 = (bf16[64,256]{1,0:T(8,128)(2,1)S(1)}, bf16[64,256]{1,0:T(8,128)(2,1)S(1)}, u32[]{:S(2)}, u32[]{:S(2)}) collective-permute-start(bf16[64,256]{1,0:T(8,128)(2,1)S(1)} %get-tuple-element.42), channel_id=1, source_target_pairs={{0,64},{16,80},{32,96},{48,112},{64,0},{80,16},{96,32},{112,48},{1... | collective-permute-start | bytes 98312 | tf_op jit(solution)/shard_map/ppermute | solution.py:30
  85.5 2.9 %collective-permute-done.22 = bf16[64,256]{1,0:T(8,128)(2,1)S(1)} collective-permute-done((bf16[64,256]{1,0:T(8,128)(2,1)S(1)}, bf16[64,256]{1,0:T(8,128)(2,1)S(1)}, u32[]{:S(2)}, u32[]{:S(2)}) %collective-permute-start.22) | collective-permute-done | bytes 32800 | tf_op jit(solution)/shard_map/ppermute | solution.py:30
  89.6 2.7 %collective-permute-start.25 = (bf16[16,1280]{1,0:T(8,128)(2,1)S(1)}, bf16[16,1280]{1,0:T(8,128)(2,1)S(1)}, u32[]{:S(2)}, u32[]{:S(2)}) collective-permute-start(bf16[16,1280]{1,0:T(8,128)(2,1)S(1)} %get-tuple-element.31), channel_id=1, source_target_pairs={{0,9},{1,8},{2,11},{3,10},{4,13},{5,12},{6,15},{7,14},{8,1},{9,0},... | collective-permute-start | bytes 122888 | tf_op jit(solution)/shard_map/ppermute | solution.py:30
  94.5 3.4 %collective-permute-start.26 = (bf16[16,1280]{1,0:T(8,128)(2,1)S(1)}, bf16[16,1280]{1,0:T(8,128)(2,1)S(1)}, u32[]{:S(2)}, u32[]{:S(2)}) collective-permute-start(bf16[16,1280]{1,0:T(8,128)(2,1)S(1)} %fusion.33), channel_id=1, source_target_pairs={{0,2},{1,3},{2,0},{3,1},{4,6},{5,7},{6,4},{7,5},{8,10},{9,11},{10,... | collective-permute-start | bytes 122888 | tf_op jit(solution)/shard_map/ppermute | solution.py:30
  97.9 5.2 %collective-permute-start.27 = (bf16[16,1280]{1,0:T(8,128)(2,1)S(1)}, bf16[16,1280]{1,0:T(8,128)(2,1)S(1)}, u32[]{:S(2)}, u32[]{:S(2)}) collective-permute-start(bf16[16,1280]{1,0:T(8,128)(2,1)S(1)} %fusion.33), channel_id=1, source_target_pairs={{0,4},{1,5},{2,6},{3,7},{4,0},{5,1},{6,2},{7,3},{8,12},{9,13},{10,... | collective-permute-start | bytes 122888 | tf_op jit(solution)/shard_map/ppermute | solution.py:30
  103.1 2.7 %collective-permute-done.27 = bf16[16,1280]{1,0:T(8,128)(2,1)S(1)} collective-permute-done((bf16[16,1280]{1,0:T(8,128)(2,1)S(1)}, bf16[16,1280]{1,0:T(8,128)(2,1)S(1)}, u32[]{:S(2)}, u32[]{:S(2)}) %collective-permute-start.27) | collective-permute-done | bytes 40992 | tf_op jit(solution)/shard_map/ppermute | solution.py:30
  105.8 3.4 %collective-permute-done.28 = bf16[16,1280]{1,0:T(8,128)(2,1)S(1)} collective-permute-done((bf16[16,1280]{1,0:T(8,128)(2,1)S(1)}, bf16[16,1280]{1,0:T(8,128)(2,1)S(1)}, u32[]{:S(2)}, u32[]{:S(2)}) %collective-permute-start.28) | collective-permute-done | bytes 40992 | tf_op jit(solution)/shard_map/ppermute | solution.py:30
  110.4 2.0 %collective-permute-start.30 = (bf16[16,1280]{1,0:T(8,128)(2,1)S(1)}, bf16[16,1280]{1,0:T(8,128)(2,1)S(1)}, u32[]{:S(2)}, u32[]{:S(2)}) collective-permute-start(bf16[16,1280]{1,0:T(8,128)(2,1)S(1)} %fusion.54), channel_id=1, source_target_pairs={{0,8},{1,9},{2,10},{3,11},{4,12},{5,13},{6,14},{7,15},{8,0},{9,1},... | collective-permute-start | bytes 122888 | tf_op jit(solution)/shard_map/ppermute | solution.py:30
  114.4 2.9 %collective-permute-done.31 = bf16[16,1280]{1,0:T(8,128)(2,1)S(1)} collective-permute-done((bf16[16,1280]{1,0:T(8,128)(2,1)S(1)}, bf16[16,1280]{1,0:T(8,128)(2,1)S(1)}, u32[]{:S(2)}, u32[]{:S(2)}) %collective-permute-start.31) | collective-permute-done | bytes 40992 | tf_op jit(solution)/shard_map/ppermute | solution.py:30
  118.0 2.9 %fusion.76 = (bf16[64,1280]{1,0:T(8,128)(2,1)}, f32[64,1280]{1,0:T(8,128)}) fusion(bf16[1280,320]{0,1:T(8,128)(2,1)} %param.17, bf16[64,1280]{1,0:T(8,128)(2,1)} %bitcast.92, bf16[320,1280]{1,0:T(8,128)(2,1)S(1)} %copy-done, f32[64,320]{1,0:T(8,128)S(1)} %fusion.4), kind=kOutput, calls=%fused_computation.122 | convolution fusion | flops 105328640 | bytes 2375680 | tf_op jit(solution)/shard_map/dot_general | solution.py:60
  129.3 5.3 %all-to-all-start.1 = ((bf16[4,4,128,256]{3,2,1,0:T(8,128)(2,1)}), bf16[4,4,128,256]{3,2,1,0:T(8,128)(2,1)S(1)}, u32[]{:S(2)}, u32[]{:S(2)}) async-start(bf16[4,4,128,256]{3,2,1,0:T(8,128)(2,1)} %bitcast.90), calls=%async_computation.1 | async-start | bytes 2097152 | tf_op jit(solution)/shard_map/all_to_all | solution.py:26
  136.1 2.5 %collective-permute-start.36 = (bf16[16,1280]{1,0:T(8,128)(2,1)S(1)}, bf16[16,1280]{1,0:T(8,128)(2,1)S(1)}, u32[]{:S(2)}, u32[]{:S(2)}) collective-permute-start(bf16[16,1280]{1,0:T(8,128)(2,1)S(1)} %fusion.31), channel_id=1, source_target_pairs={{0,4},{1,5},{2,6},{3,7},{4,0},{5,1},{6,2},{7,3},{8,12},{9,13},{10,... | collective-permute-start | bytes 122888 | tf_op jit(solution)/shard_map/ppermute | solution.py:30
  138.6 3.5 %collective-permute-start.37 = (bf16[16,1280]{1,0:T(8,128)(2,1)S(1)}, bf16[16,1280]{1,0:T(8,128)(2,1)S(1)}, u32[]{:S(2)}, u32[]{:S(2)}) collective-permute-start(bf16[16,1280]{1,0:T(8,128)(2,1)S(1)} %fusion.31), channel_id=1, source_target_pairs={{0,6},{1,7},{2,4},{3,5},{4,2},{5,3},{6,0},{7,1},{8,14},{9,15},{10,... | collective-permute-start | bytes 122888 | tf_op jit(solution)/shard_map/ppermute | solution.py:30
  143.8 1.9 %collective-permute-done.36 = bf16[16,1280]{1,0:T(8,128)(2,1)S(1)} collective-permute-done((bf16[16,1280]{1,0:T(8,128)(2,1)S(1)}, bf16[16,1280]{1,0:T(8,128)(2,1)S(1)}, u32[]{:S(2)}, u32[]{:S(2)}) %collective-permute-start.36) | collective-permute-done | bytes 40992 | tf_op jit(solution)/shard_map/ppermute | solution.py:30
  146.2 2.2 %collective-permute-start.39 = (bf16[16,1280]{1,0:T(8,128)(2,1)S(1)}, bf16[16,1280]{1,0:T(8,128)(2,1)S(1)}, u32[]{:S(2)}, u32[]{:S(2)}) collective-permute-start(bf16[16,1280]{1,0:T(8,128)(2,1)S(1)} %add_convert_fusion.2), channel_id=1, source_target_pairs={{0,8},{1,9},{2,10},{3,11},{4,12},{5,13},{6,14},{7,15},{8,0},{9,1},... | collective-permute-start | bytes 122888 | tf_op jit(solution)/shard_map/ppermute | solution.py:30
  150.3 3.6 %collective-permute-done.40 = bf16[16,1280]{1,0:T(8,128)(2,1)S(1)} collective-permute-done((bf16[16,1280]{1,0:T(8,128)(2,1)S(1)}, bf16[16,1280]{1,0:T(8,128)(2,1)S(1)}, u32[]{:S(2)}, u32[]{:S(2)}) %collective-permute-start.40) | collective-permute-done | bytes 40992 | tf_op jit(solution)/shard_map/ppermute | solution.py:30
  154.4 5.8 %collective-permute-done.16 = bf16[2,128,256]{2,1,0:T(8,128)(2,1)S(1)} collective-permute-done((bf16[2,128,256]{2,1,0:T(8,128)(2,1)S(1)}, bf16[2,128,256]{2,1,0:T(8,128)(2,1)S(1)}, u32[]{:S(2)}, u32[]{:S(2)}) %collective-permute-start.16) | collective-permute-done | bytes 131104 | tf_op jit(solution)/shard_map/ppermute | solution.py:30
  160.2 3.2 %collective-permute-start.17 = (bf16[128,256]{1,0:T(8,128)(2,1)S(1)}, bf16[128,256]{1,0:T(8,128)(2,1)S(1)}, u32[]{:S(2)}, u32[]{:S(2)}) collective-permute-start(bf16[128,256]{1,0:T(8,128)(2,1)S(1)} %fusion.38), channel_id=1, source_target_pairs={{0,6},{1,7},{2,4},{3,5},{4,2},{5,3},{6,0},{7,1},{8,14},{9,15},{10,... | collective-permute-start | bytes 196616 | tf_op jit(solution)/shard_map/ppermute | solution.py:30
  164.2 2.5 %collective-permute-done.17 = bf16[128,256]{1,0:T(8,128)(2,1)S(1)} collective-permute-done((bf16[128,256]{1,0:T(8,128)(2,1)S(1)}, bf16[128,256]{1,0:T(8,128)(2,1)S(1)}, u32[]{:S(2)}, u32[]{:S(2)}) %collective-permute-start.17) | collective-permute-done | bytes 65568 | tf_op jit(solution)/shard_map/ppermute | solution.py:30
  (132 shorter events, 54.4 us)
Async XLA Ops:
  4.2 30.9 %all-to-all-start = ((bf16[4,1024,256]{2,1,0:T(8,128)(2,1)}), bf16[4,1024,256]{2,1,0:T(8,128)(2,1)S(1)}, u32[]{:S(2)}, u32[]{:S(2)}) async-start(bf16[4,1024,256]{2,1,0:T(8,128)(2,1)} %copy-done.1), calls=%async_computation | async-start | bytes 4194304 | tf_op jit(solution)/shard_map/all_to_all | solution.py:26
  14.7 4.9 %collective-permute-start.3 = (bf16[16,1280]{1,0:T(8,128)(2,1)S(1)}, bf16[16,1280]{1,0:T(8,128)(2,1)S(1)}, u32[]{:S(2)}, u32[]{:S(2)}) collective-permute-start(bf16[16,1280]{1,0:T(8,128)(2,1)S(1)} %get-tuple-element.34), channel_id=1, source_target_pairs={{0,9},{1,8},{2,11},{3,10},{4,13},{5,12},{6,15},{7,14},{8,1},{9,0},... | collective-permute-start | bytes 122888 | tf_op jit(solution)/shard_map/ppermute | solution.py:30
  19.6 16.7 %collective-permute-start.4 = (bf16[16,1280]{1,0:T(8,128)(2,1)S(1)}, bf16[16,1280]{1,0:T(8,128)(2,1)S(1)}, u32[]{:S(2)}, u32[]{:S(2)}) collective-permute-start(bf16[16,1280]{1,0:T(8,128)(2,1)S(1)} %fusion.35), channel_id=1, source_target_pairs={{0,2},{1,3},{2,0},{3,1},{4,6},{5,7},{6,4},{7,5},{8,10},{9,11},{10,... | collective-permute-start | bytes 122888 | tf_op jit(solution)/shard_map/ppermute | solution.py:30
  23.0 13.4 %collective-permute-start.5 = (bf16[16,1280]{1,0:T(8,128)(2,1)S(1)}, bf16[16,1280]{1,0:T(8,128)(2,1)S(1)}, u32[]{:S(2)}, u32[]{:S(2)}) collective-permute-start(bf16[16,1280]{1,0:T(8,128)(2,1)S(1)} %fusion.35), channel_id=1, source_target_pairs={{0,4},{1,5},{2,6},{3,7},{4,0},{5,1},{6,2},{7,3},{8,12},{9,13},{10,... | collective-permute-start | bytes 122888 | tf_op jit(solution)/shard_map/ppermute | solution.py:30
  28.4 8.0 %collective-permute-start.6 = (bf16[16,1280]{1,0:T(8,128)(2,1)S(1)}, bf16[16,1280]{1,0:T(8,128)(2,1)S(1)}, u32[]{:S(2)}, u32[]{:S(2)}) collective-permute-start(bf16[16,1280]{1,0:T(8,128)(2,1)S(1)} %fusion.35), channel_id=1, source_target_pairs={{0,6},{1,7},{2,4},{3,5},{4,2},{5,3},{6,0},{7,1},{8,14},{9,15},{10,... | collective-permute-start | bytes 122888 | tf_op jit(solution)/shard_map/ppermute | solution.py:30
  35.1 30.6 %collective-permute-start = (bf16[4,1024,256]{2,1,0:T(8,128)(2,1)S(1)}, bf16[4,1024,256]{2,1,0:T(8,128)(2,1)S(1)}, u32[]{:S(2)}, u32[]{:S(2)}) collective-permute-start(bf16[4,1024,256]{2,1,0:T(8,128)(2,1)S(1)} %all-to-all-done.own), channel_id=1, source_target_pairs={{0,16},{16,0},{32,48},{48,32},{64,80},{80,64},{96,112},{112,96},{1... | collective-permute-start | bytes 6291464 | tf_op jit(solution)/shard_map/ppermute | solution.py:30
  36.2 12.9 %collective-permute-start.10 = (bf16[2,1280,64]{1,2,0:T(8,128)(2,1)S(1)}, bf16[2,1280,64]{1,2,0:T(8,128)(2,1)S(1)}, u32[]{:S(2)}, u32[]{:S(2)}) collective-permute-start(bf16[2,1280,64]{1,2,0:T(8,128)(2,1)S(1)} %pad_maximum_fusion.1), channel_id=1, source_target_pairs={{0,1},{1,0},{2,3},{3,2},{4,5},{5,4},{6,7},{7,6},{8,9},{9,8},{10,11... | collective-permute-start | bytes 983048 | tf_op jit(solution)/shard_map/ppermute | solution.py:30
  37.3 10.4 %collective-permute-start.7 = (bf16[16,1280]{1,0:T(8,128)(2,1)S(1)}, bf16[16,1280]{1,0:T(8,128)(2,1)S(1)}, u32[]{:S(2)}, u32[]{:S(2)}) collective-permute-start(bf16[16,1280]{1,0:T(8,128)(2,1)S(1)} %fusion.37), channel_id=1, source_target_pairs={{0,1},{1,0},{2,3},{3,2},{4,5},{5,4},{6,7},{7,6},{8,9},{9,8},{10,11... | collective-permute-start | bytes 122888 | tf_op jit(solution)/shard_map/ppermute | solution.py:30
  39.3 8.4 %collective-permute-start.8 = (bf16[16,1280]{1,0:T(8,128)(2,1)S(1)}, bf16[16,1280]{1,0:T(8,128)(2,1)S(1)}, u32[]{:S(2)}, u32[]{:S(2)}) collective-permute-start(bf16[16,1280]{1,0:T(8,128)(2,1)S(1)} %fusion.37), channel_id=1, source_target_pairs={{0,8},{1,9},{2,10},{3,11},{4,12},{5,13},{6,14},{7,15},{8,0},{9,1},... | collective-permute-start | bytes 122888 | tf_op jit(solution)/shard_map/ppermute | solution.py:30
  40.8 8.3 %collective-permute-start.9 = (bf16[16,1280]{1,0:T(8,128)(2,1)S(1)}, bf16[16,1280]{1,0:T(8,128)(2,1)S(1)}, u32[]{:S(2)}, u32[]{:S(2)}) collective-permute-start(bf16[16,1280]{1,0:T(8,128)(2,1)S(1)} %fusion.37), channel_id=1, source_target_pairs={{0,9},{1,8},{2,11},{3,10},{4,13},{5,12},{6,15},{7,14},{8,1},{9,0},... | collective-permute-start | bytes 122888 | tf_op jit(solution)/shard_map/ppermute | solution.py:30
  50.4 5.5 %collective-permute-start.11 = (bf16[64,256]{1,0:T(8,128)(2,1)S(1)}, bf16[64,256]{1,0:T(8,128)(2,1)S(1)}, u32[]{:S(2)}, u32[]{:S(2)}) collective-permute-start(bf16[64,256]{1,0:T(8,128)(2,1)S(1)} %convolution_convert_fusion), channel_id=1, source_target_pairs={{0,128},{128,0},{1,129},{129,1},{2,130},{130,2},{3,131},{131,3},{4... | collective-permute-start | bytes 98312 | tf_op jit(solution)/shard_map/ppermute | solution.py:30
  56.6 5.8 %collective-permute-start.13 = (bf16[2,64,256]{2,1,0:T(8,128)(2,1)S(1)}, bf16[2,64,256]{2,1,0:T(8,128)(2,1)S(1)}, u32[]{:S(2)}, u32[]{:S(2)}) collective-permute-start(bf16[2,64,256]{2,1,0:T(8,128)(2,1)S(1)} %get-tuple-element.44), channel_id=1, source_target_pairs={{0,64},{16,80},{32,96},{48,112},{64,0},{80,16},{96,32},{112,48},{1... | collective-permute-start | bytes 196616 | tf_op jit(solution)/shard_map/ppermute | solution.py:30
  58.7 5.5 %collective-permute-start.14 = (bf16[2,64,256]{2,1,0:T(8,128)(2,1)S(1)}, bf16[2,64,256]{2,1,0:T(8,128)(2,1)S(1)}, u32[]{:S(2)}, u32[]{:S(2)}) collective-permute-start(bf16[2,64,256]{2,1,0:T(8,128)(2,1)S(1)} %get-tuple-element.44), channel_id=1, source_target_pairs={{0,96},{16,112},{32,64},{48,80},{64,32},{80,48},{96,0},{112,16},{1... | collective-permute-start | bytes 196616 | tf_op jit(solution)/shard_map/ppermute | solution.py:30
  64.2 5.1 %collective-permute-start.15 = (bf16[4,2,64,256]{3,2,1,0:T(8,128)(2,1)S(1)}, bf16[4,2,64,256]{3,2,1,0:T(8,128)(2,1)S(1)}, u32[]{:S(2)}, u32[]{:S(2)}) collective-permute-start(bf16[4,2,64,256]{3,2,1,0:T(8,128)(2,1)S(1)} %pad_maximum_fusion.2.own), channel_id=1, source_target_pairs={{0,16},{16,0},{32,48},{48,32},{64,80},{80,64},{96,112},{112,96},{1... | collective-permute-start | bytes 786440 | tf_op jit(solution)/shard_map/ppermute | solution.py:30
  72.2 7.4 %collective-permute-start.19 = (bf16[4,64,256]{2,1,0:T(8,128)(2,1)S(1)}, bf16[4,64,256]{2,1,0:T(8,128)(2,1)S(1)}, u32[]{:S(2)}, u32[]{:S(2)}) collective-permute-start(bf16[4,64,256]{2,1,0:T(8,128)(2,1)S(1)} %fusion.7), channel_id=1, source_target_pairs={{0,128},{128,0},{1,129},{129,1},{2,130},{130,2},{3,131},{131,3},{4... | collective-permute-start | bytes 393224 | tf_op jit(solution)/shard_map/ppermute | solution.py:30
  79.8 5.8 %collective-permute-start.21 = (bf16[64,256]{1,0:T(8,128)(2,1)S(1)}, bf16[64,256]{1,0:T(8,128)(2,1)S(1)}, u32[]{:S(2)}, u32[]{:S(2)}) collective-permute-start(bf16[64,256]{1,0:T(8,128)(2,1)S(1)} %get-tuple-element.42), channel_id=1, source_target_pairs={{0,64},{16,80},{32,96},{48,112},{64,0},{80,16},{96,32},{112,48},{1... | collective-permute-start | bytes 98312 | tf_op jit(solution)/shard_map/ppermute | solution.py:30
  83.3 5.1 %collective-permute-start.22 = (bf16[64,256]{1,0:T(8,128)(2,1)S(1)}, bf16[64,256]{1,0:T(8,128)(2,1)S(1)}, u32[]{:S(2)}, u32[]{:S(2)}) collective-permute-start(bf16[64,256]{1,0:T(8,128)(2,1)S(1)} %get-tuple-element.41), channel_id=1, source_target_pairs={{0,96},{16,112},{32,64},{48,80},{64,32},{80,48},{96,0},{112,16},{1... | collective-permute-start | bytes 98312 | tf_op jit(solution)/shard_map/ppermute | solution.py:30
  89.6 4.9 %collective-permute-start.25 = (bf16[16,1280]{1,0:T(8,128)(2,1)S(1)}, bf16[16,1280]{1,0:T(8,128)(2,1)S(1)}, u32[]{:S(2)}, u32[]{:S(2)}) collective-permute-start(bf16[16,1280]{1,0:T(8,128)(2,1)S(1)} %get-tuple-element.31), channel_id=1, source_target_pairs={{0,9},{1,8},{2,11},{3,10},{4,13},{5,12},{6,15},{7,14},{8,1},{9,0},... | collective-permute-start | bytes 122888 | tf_op jit(solution)/shard_map/ppermute | solution.py:30
  94.5 8.6 %collective-permute-start.26 = (bf16[16,1280]{1,0:T(8,128)(2,1)S(1)}, bf16[16,1280]{1,0:T(8,128)(2,1)S(1)}, u32[]{:S(2)}, u32[]{:S(2)}) collective-permute-start(bf16[16,1280]{1,0:T(8,128)(2,1)S(1)} %fusion.33), channel_id=1, source_target_pairs={{0,2},{1,3},{2,0},{3,1},{4,6},{5,7},{6,4},{7,5},{8,10},{9,11},{10,... | collective-permute-start | bytes 122888 | tf_op jit(solution)/shard_map/ppermute | solution.py:30
  97.9 7.9 %collective-permute-start.27 = (bf16[16,1280]{1,0:T(8,128)(2,1)S(1)}, bf16[16,1280]{1,0:T(8,128)(2,1)S(1)}, u32[]{:S(2)}, u32[]{:S(2)}) collective-permute-start(bf16[16,1280]{1,0:T(8,128)(2,1)S(1)} %fusion.33), channel_id=1, source_target_pairs={{0,4},{1,5},{2,6},{3,7},{4,0},{5,1},{6,2},{7,3},{8,12},{9,13},{10,... | collective-permute-start | bytes 122888 | tf_op jit(solution)/shard_map/ppermute | solution.py:30
  103.1 6.1 %collective-permute-start.28 = (bf16[16,1280]{1,0:T(8,128)(2,1)S(1)}, bf16[16,1280]{1,0:T(8,128)(2,1)S(1)}, u32[]{:S(2)}, u32[]{:S(2)}) collective-permute-start(bf16[16,1280]{1,0:T(8,128)(2,1)S(1)} %fusion.33), channel_id=1, source_target_pairs={{0,6},{1,7},{2,4},{3,5},{4,2},{5,3},{6,0},{7,1},{8,14},{9,15},{10,... | collective-permute-start | bytes 122888 | tf_op jit(solution)/shard_map/ppermute | solution.py:30
  112.4 5.0 %collective-permute-start.31 = (bf16[16,1280]{1,0:T(8,128)(2,1)S(1)}, bf16[16,1280]{1,0:T(8,128)(2,1)S(1)}, u32[]{:S(2)}, u32[]{:S(2)}) collective-permute-start(bf16[16,1280]{1,0:T(8,128)(2,1)S(1)} %fusion.54), channel_id=1, source_target_pairs={{0,9},{1,8},{2,11},{3,10},{4,13},{5,12},{6,15},{7,14},{8,1},{9,0},... | collective-permute-start | bytes 122888 | tf_op jit(solution)/shard_map/ppermute | solution.py:30
  122.3 12.3 %collective-permute-start.32 = (bf16[16,1280]{1,0:T(8,128)(2,1)}, bf16[16,1280]{1,0:T(8,128)(2,1)S(1)}, u32[]{:S(2)}, u32[]{:S(2)}) collective-permute-start(bf16[16,1280]{1,0:T(8,128)(2,1)} %get-tuple-element.27), channel_id=1, source_target_pairs={{0,1},{1,0},{2,3},{3,2},{4,5},{5,4},{6,7},{7,6},{8,9},{9,8},{10,11... | collective-permute-start | bytes 122888 | tf_op jit(solution)/shard_map/ppermute | solution.py:30
  124.1 10.6 %collective-permute-start.33 = (bf16[16,1280]{1,0:T(8,128)(2,1)}, bf16[16,1280]{1,0:T(8,128)(2,1)}, u32[]{:S(2)}, u32[]{:S(2)}) collective-permute-start(bf16[16,1280]{1,0:T(8,128)(2,1)} %get-tuple-element.29), channel_id=1, source_target_pairs={{0,8},{1,9},{2,10},{3,11},{4,12},{5,13},{6,14},{7,15},{8,0},{9,1},... | collective-permute-start | bytes 122888 | tf_op jit(solution)/shard_map/ppermute | solution.py:30
  124.1 10.6 %collective-permute-start.34 = (bf16[16,1280]{1,0:T(8,128)(2,1)S(1)}, bf16[16,1280]{1,0:T(8,128)(2,1)}, u32[]{:S(2)}, u32[]{:S(2)}) collective-permute-start(bf16[16,1280]{1,0:T(8,128)(2,1)S(1)} %get-tuple-element.28), channel_id=1, source_target_pairs={{0,9},{1,8},{2,11},{3,10},{4,13},{5,12},{6,15},{7,14},{8,1},{9,0},... | collective-permute-start | bytes 122888 | tf_op jit(solution)/shard_map/ppermute | solution.py:30
  129.3 24.7 %all-to-all-start.1 = ((bf16[4,4,128,256]{3,2,1,0:T(8,128)(2,1)}), bf16[4,4,128,256]{3,2,1,0:T(8,128)(2,1)S(1)}, u32[]{:S(2)}, u32[]{:S(2)}) async-start(bf16[4,4,128,256]{3,2,1,0:T(8,128)(2,1)} %bitcast.90), calls=%async_computation.1 | async-start | bytes 2097152 | tf_op jit(solution)/shard_map/all_to_all | solution.py:26
  135.6 8.2 %collective-permute-start.35 = (bf16[16,1280]{1,0:T(8,128)(2,1)S(1)}, bf16[16,1280]{1,0:T(8,128)(2,1)S(1)}, u32[]{:S(2)}, u32[]{:S(2)}) collective-permute-start(bf16[16,1280]{1,0:T(8,128)(2,1)S(1)} %fusion.31), channel_id=1, source_target_pairs={{0,2},{1,3},{2,0},{3,1},{4,6},{5,7},{6,4},{7,5},{8,10},{9,11},{10,... | collective-permute-start | bytes 122888 | tf_op jit(solution)/shard_map/ppermute | solution.py:30
  136.1 9.6 %collective-permute-start.36 = (bf16[16,1280]{1,0:T(8,128)(2,1)S(1)}, bf16[16,1280]{1,0:T(8,128)(2,1)S(1)}, u32[]{:S(2)}, u32[]{:S(2)}) collective-permute-start(bf16[16,1280]{1,0:T(8,128)(2,1)S(1)} %fusion.31), channel_id=1, source_target_pairs={{0,4},{1,5},{2,6},{3,7},{4,0},{5,1},{6,2},{7,3},{8,12},{9,13},{10,... | collective-permute-start | bytes 122888 | tf_op jit(solution)/shard_map/ppermute | solution.py:30
  138.6 7.1 %collective-permute-start.37 = (bf16[16,1280]{1,0:T(8,128)(2,1)S(1)}, bf16[16,1280]{1,0:T(8,128)(2,1)S(1)}, u32[]{:S(2)}, u32[]{:S(2)}) collective-permute-start(bf16[16,1280]{1,0:T(8,128)(2,1)S(1)} %fusion.31), channel_id=1, source_target_pairs={{0,6},{1,7},{2,4},{3,5},{4,2},{5,3},{6,0},{7,1},{8,14},{9,15},{10,... | collective-permute-start | bytes 122888 | tf_op jit(solution)/shard_map/ppermute | solution.py:30
  148.4 5.6 %collective-permute-start.40 = (bf16[16,1280]{1,0:T(8,128)(2,1)S(1)}, bf16[16,1280]{1,0:T(8,128)(2,1)S(1)}, u32[]{:S(2)}, u32[]{:S(2)}) collective-permute-start(bf16[16,1280]{1,0:T(8,128)(2,1)S(1)} %add_convert_fusion.2), channel_id=1, source_target_pairs={{0,9},{1,8},{2,11},{3,10},{4,13},{5,12},{6,15},{7,14},{8,1},{9,0},... | collective-permute-start | bytes 122888 | tf_op jit(solution)/shard_map/ppermute | solution.py:30
  154.1 6.1 %collective-permute-start.16 = (bf16[2,128,256]{2,1,0:T(8,128)(2,1)S(1)}, bf16[2,128,256]{2,1,0:T(8,128)(2,1)S(1)}, u32[]{:S(2)}, u32[]{:S(2)}) collective-permute-start(bf16[2,128,256]{2,1,0:T(8,128)(2,1)S(1)} %get-tuple-element.13), channel_id=1, source_target_pairs={{0,2},{1,3},{2,0},{3,1},{4,6},{5,7},{6,4},{7,5},{8,10},{9,11},{10,... | collective-permute-start | bytes 393224 | tf_op jit(solution)/shard_map/ppermute | solution.py:30
  160.2 6.5 %collective-permute-start.17 = (bf16[128,256]{1,0:T(8,128)(2,1)S(1)}, bf16[128,256]{1,0:T(8,128)(2,1)S(1)}, u32[]{:S(2)}, u32[]{:S(2)}) collective-permute-start(bf16[128,256]{1,0:T(8,128)(2,1)S(1)} %fusion.38), channel_id=1, source_target_pairs={{0,6},{1,7},{2,4},{3,5},{4,2},{5,3},{6,0},{7,1},{8,14},{9,15},{10,... | collective-permute-start | bytes 196616 | tf_op jit(solution)/shard_map/ppermute | solution.py:30
  (26 other events, 153.5 us)
where the time goes:
time: 171 us; the launch traced here: 168 us
  starting transfers between devices  75.4 us (44%)
  waiting for transfers between devices  62.3 us (36%)
  other arithmetic  8.53 us (5%)
  local copies, waits for them, and re-layouts  7.7 us (5%)
  matrix products  6.19 us (4%)
  Pallas kernels  5.71 us (3%)
  between operations  2.38 us (1%)
    ppermute x41, starting transfers between devices, swapped(): lax.ppermute(x, axis, [(i, i ^ mask) for i in range(lax.axis_size(axis))])  65.5 us
    ppermute x41, waiting for transfers between devices, swapped(): lax.ppermute(x, axis, [(i, i ^ mask) for i in range(lax.axis_size(axis))])  55.6 us
    all_to_all x2, starting transfers between devices, exchanged(): return lax.all_to_all(x, axis, 0, 0, tiled=True, axis_index_groups=groups)  9.92 us
    all_to_all x2, waiting for transfers between devices, exchanged(): return lax.all_to_all(x, axis, 0, 0, tiled=True, axis_index_groups=groups)  6.75 us
    unnamed x30, local copies, waits for them, and re-layouts  5.96 us
    pallas_call x1, Pallas kernels, shards(): pl.pallas_call(text_kernel, out_shape=(small, small), in_specs=[SMEM] + [...  3.43 us
  transfers between devices with their start and end apart: 43, of which 27 were waited for; matrix products, arithmetic and copies ran while one was open for 6% of the time, Pallas kernels for 3%

commit v1 on v0

--- a/solution.py
+++ b/solution.py
@@ -14,6 +14,8 @@
 
 NEAR = (1, 8, 9)
 FAR = (4, 2, 6)
+FARTHEST_NEAR = (3, 1, 2)
+FARTHEST_Y = (2, 1, 3)
 NEAR_SETS = [[b, b + 1, b + 8, b + 9] for b in (0, 2, 4, 6)]
 ALONG_Y = [[0, 2, 4, 6], [1, 3, 5, 7]]
 
@@ -61,14 +63,15 @@
 
 
 def reduced_chunk(term):
-    near = [swapped(term[k].astype(BF16), "mp", NEAR[k - 1]).astype(F32) for k in (1, 2, 3)]
-    part = ((term[0] + near[0]) + (near[1] + near[2])).astype(BF16)
+    near = {k: swapped(term[k].astype(BF16), "mp", NEAR[k - 1]).astype(F32) for k in FARTHEST_NEAR}
+    part = ((term[0] + near[1]) + (near[2] + near[3])).astype(BF16)
     far = [swapped(part, "mp", mask).astype(F32) for mask in FAR]
     return (part.astype(F32) + far[1]) + (far[0] + far[2])
 
 
 def gathered_chunks(chunk):
-    return jnp.stack([chunk] + [swapped(chunk, "mp", mask) for mask in NEAR])
+    near = {k: swapped(chunk, "mp", NEAR[k - 1]) for k in FARTHEST_NEAR}
+    return jnp.stack([chunk, near[1], near[2], near[3]])
 
 
 def spread_kernel(first, second, out, held, sems):
@@ -232,7 +235,8 @@
     kv_cols = jnp.concatenate([key_proj, partner_kv[0], value_proj, partner_kv[1]], axis=1)
     local_kv = jnp.dot(image_state, kv_cols, preferred_element_type=F32).astype(BF16)
     both = jnp.stack([local_kv, swapped(local_kv, "group", 1)])
-    own_core = jnp.stack([both] + [swapped(both, "seq", 2 * k) for k in (1, 2, 3)])
+    by_y = {k: swapped(both, "seq", 2 * k) for k in FARTHEST_Y}
+    own_core = jnp.stack([both, by_y[1], by_y[2], by_y[3]])
     other_core = swapped(own_core, "seq", 1)
 
     small = jax.ShapeDtypeStruct((text_rows, head_cols), BF16)
@@ -265,8 +269,8 @@
 
     summed = grads_own.astype(F32) + swapped(grads_other, "seq", 1).astype(F32)
     summed = summed[0] + swapped(summed[1].astype(BF16), "group", 1).astype(F32)
-    along_y = [swapped(summed[k].astype(BF16), "seq", 2 * k).astype(F32) for k in (1, 2, 3)]
-    kv_grads = (summed[0] + along_y[0]) + (along_y[1] + along_y[2])
+    along_y = {k: swapped(summed[k].astype(BF16), "seq", 2 * k).astype(F32) for k in FARTHEST_Y}
+    kv_grads = (summed[0] + along_y[1]) + (along_y[2] + along_y[3])
     state_term = contract_last(kv_grads.astype(BF16), kv_cols)
     state_chunk_grad = reduced_chunk(state_term.reshape(4, chunk_rows, vision_width))
     state_half = gathered_chunks(state_chunk_grad.astype(BF16)).reshape(image_rows, vision_width)

time: 171 us -> 171 us (level)
  no operation moved by 1% of the time
where the time goes in v1:
time: 171 us; the launch traced here: 168 us
  starting transfers between devices  75.4 us (44%)
  waiting for transfers between devices  62.3 us (36%)
  other arithmetic  8.53 us (5%)
  local copies, waits for them, and re-layouts  7.7 us (5%)
  matrix products  6.19 us (4%)
  Pallas kernels  5.71 us (3%)
  between operations  2.38 us (1%)
    ppermute x41, starting transfers between devices, swapped(): lax.ppermute(x, axis, [(i, i ^ mask) for i in range(lax.axis_size(axis))])  65.5 us
    ppermute x41, waiting for transfers between devices, swapped(): lax.ppermute(x, axis, [(i, i ^ mask) for i in range(lax.axis_size(axis))])  55.6 us
    all_to_all x2, starting transfers between devices, exchanged(): return lax.all_to_all(x, axis, 0, 0, tiled=True, axis_index_groups=groups)  9.92 us
    all_to_all x2, waiting for transfers between devices, exchanged(): return lax.all_to_all(x, axis, 0, 0, tiled=True, axis_index_groups=groups)  6.75 us
    unnamed x30, local copies, waits for them, and re-layouts  5.96 us
    pallas_call x1, Pallas kernels, shards(): pl.pallas_call(text_kernel, out_shape=(small, small), in_specs=[SMEM] + [...  3.43 us
  transfers between devices with their start and end apart: 43, of which 27 were waited for; matrix products, arithmetic and copies ran while one was open for 6% of the time, Pallas kernels for 3%

profile of v1, /device:TPU:32, one launch (start us, length us, event | category | flops | bytes accessed | tf_op | source)
XLA Modules:
  0.0 168.2 jit_solution(17100460118534911524)
XLA Ops:
  4.2 4.6 %all-to-all-start = ((bf16[4,1024,256]{2,1,0:T(8,128)(2,1)}), bf16[4,1024,256]{2,1,0:T(8,128)(2,1)S(1)}, u32[]{:S(2)}, u32[]{:S(2)}) async-start(bf16[4,1024,256]{2,1,0:T(8,128)(2,1)} %copy-done.1), calls=%async_computation | async-start | bytes 4194304 | tf_op jit(solution)/shard_map/all_to_all | solution.py:28
  19.6 3.4 %collective-permute-start.4 = (bf16[16,1280]{1,0:T(8,128)(2,1)S(1)}, bf16[16,1280]{1,0:T(8,128)(2,1)S(1)}, u32[]{:S(2)}, u32[]{:S(2)}) collective-permute-start(bf16[16,1280]{1,0:T(8,128)(2,1)S(1)} %fusion.35), channel_id=1, source_target_pairs={{0,2},{1,3},{2,0},{3,1},{4,6},{5,7},{6,4},{7,5},{8,10},{9,11},{10,... | collective-permute-start | bytes 122888 | tf_op jit(solution)/shard_map/ppermute | solution.py:32
  23.0 5.4 %collective-permute-start.5 = (bf16[16,1280]{1,0:T(8,128)(2,1)S(1)}, bf16[16,1280]{1,0:T(8,128)(2,1)S(1)}, u32[]{:S(2)}, u32[]{:S(2)}) collective-permute-start(bf16[16,1280]{1,0:T(8,128)(2,1)S(1)} %fusion.35), channel_id=1, source_target_pairs={{0,4},{1,5},{2,6},{3,7},{4,0},{5,1},{6,2},{7,3},{8,12},{9,13},{10,... | collective-permute-start | bytes 122888 | tf_op jit(solution)/shard_map/ppermute | solution.py:32
  28.4 6.7 %all-to-all-done.own = bf16[4,1024,256]{2,1,0:T(8,128)(2,1)S(1)} async-done(((bf16[4,1024,256]{2,1,0:T(8,128)(2,1)}), bf16[4,1024,256]{2,1,0:T(8,128)(2,1)S(1)}, u32[]{:S(2)}, u32[]{:S(2)}) %all-to-all-start) | async-done | bytes 2097184 | tf_op jit(solution)/shard_map/all_to_all | solution.py:28
  37.3 2.0 %collective-permute-start.7 = (bf16[16,1280]{1,0:T(8,128)(2,1)S(1)}, bf16[16,1280]{1,0:T(8,128)(2,1)S(1)}, u32[]{:S(2)}, u32[]{:S(2)}) collective-permute-start(bf16[16,1280]{1,0:T(8,128)(2,1)S(1)} %fusion.37), channel_id=1, source_target_pairs={{0,1},{1,0},{2,3},{3,2},{4,5},{5,4},{6,7},{7,6},{8,9},{9,8},{10,11... | collective-permute-start | bytes 122888 | tf_op jit(solution)/shard_map/ppermute | solution.py:32
  40.9 6.8 %collective-permute-done.7 = bf16[16,1280]{1,0:T(8,128)(2,1)S(1)} collective-permute-done((bf16[16,1280]{1,0:T(8,128)(2,1)S(1)}, bf16[16,1280]{1,0:T(8,128)(2,1)S(1)}, u32[]{:S(2)}, u32[]{:S(2)}) %collective-permute-start.7) | collective-permute-done | bytes 40992 | tf_op jit(solution)/shard_map/ppermute | solution.py:32
  50.4 2.8 %collective-permute-start.11 = (bf16[64,256]{1,0:T(8,128)(2,1)S(1)}, bf16[64,256]{1,0:T(8,128)(2,1)S(1)}, u32[]{:S(2)}, u32[]{:S(2)}) collective-permute-start(bf16[64,256]{1,0:T(8,128)(2,1)S(1)} %convolution_convert_fusion), channel_id=1, source_target_pairs={{0,128},{128,0},{1,129},{129,1},{2,130},{130,2},{3,131},{131,3},{4... | collective-permute-start | bytes 98312 | tf_op jit(solution)/shard_map/ppermute | solution.py:32
  53.3 2.7 %collective-permute-done.11 = bf16[64,256]{1,0:T(8,128)(2,1)S(1)} collective-permute-done((bf16[64,256]{1,0:T(8,128)(2,1)S(1)}, bf16[64,256]{1,0:T(8,128)(2,1)S(1)}, u32[]{:S(2)}, u32[]{:S(2)}) %collective-permute-start.11) | collective-permute-done | bytes 32800 | tf_op jit(solution)/shard_map/ppermute | solution.py:32
  56.6 2.1 %collective-permute-start.13 = (bf16[2,64,256]{2,1,0:T(8,128)(2,1)S(1)}, bf16[2,64,256]{2,1,0:T(8,128)(2,1)S(1)}, u32[]{:S(2)}, u32[]{:S(2)}) collective-permute-start(bf16[2,64,256]{2,1,0:T(8,128)(2,1)S(1)} %get-tuple-element.44), channel_id=1, source_target_pairs={{0,64},{16,80},{32,96},{48,112},{64,0},{80,16},{96,32},{112,48},{1... | collective-permute-start | bytes 196616 | tf_op jit(solution)/shard_map/ppermute | solution.py:32
  58.7 2.1 %collective-permute-start.14 = (bf16[2,64,256]{2,1,0:T(8,128)(2,1)S(1)}, bf16[2,64,256]{2,1,0:T(8,128)(2,1)S(1)}, u32[]{:S(2)}, u32[]{:S(2)}) collective-permute-start(bf16[2,64,256]{2,1,0:T(8,128)(2,1)S(1)} %get-tuple-element.44), channel_id=1, source_target_pairs={{0,96},{16,112},{32,64},{48,80},{64,32},{80,48},{96,0},{112,16},{1... | collective-permute-start | bytes 196616 | tf_op jit(solution)/shard_map/ppermute | solution.py:32
  65.8 3.4 %text_projections.1 = (bf16[128,256]{1,0:T(8,128)(2,1)S(1)}, bf16[128,256]{1,0:T(8,128)(2,1)S(1)}) custom-call(s32[1]{0:T(128)S(6)} %copy.17.doc, f32[1,1]{1,0:T(1,128)} %bitcast.89.gate, f32[1,4096]{1,0:T(1,128)S(1)} %bitcast.91, bf16[4,1024,256]{2,1,0:T(8,128)(2,1)S(1)} %all-to-all-done.own, bf16[4,1024,256]{2,1,0:T(8,128)(2,1)S(1)} %collective-permute-done.other, ...), custom_call_target="tpu_custom_call" | custom-call | tf_op jit(solution)/shard_map/text_projections/pallas_call | solution.py:244
  72.2 2.8 %collective-permute-start.19 = (bf16[4,64,256]{2,1,0:T(8,128)(2,1)S(1)}, bf16[4,64,256]{2,1,0:T(8,128)(2,1)S(1)}, u32[]{:S(2)}, u32[]{:S(2)}) collective-permute-start(bf16[4,64,256]{2,1,0:T(8,128)(2,1)S(1)} %fusion.7), channel_id=1, source_target_pairs={{0,128},{128,0},{1,129},{129,1},{2,130},{130,2},{3,131},{131,3},{4... | collective-permute-start | bytes 393224 | tf_op jit(solution)/shard_map/ppermute | solution.py:32
  75.1 4.5 %collective-permute-done.19 = bf16[4,64,256]{2,1,0:T(8,128)(2,1)S(1)} collective-permute-done((bf16[4,64,256]{2,1,0:T(8,128)(2,1)S(1)}, bf16[4,64,256]{2,1,0:T(8,128)(2,1)S(1)}, u32[]{:S(2)}, u32[]{:S(2)}) %collective-permute-start.19) | collective-permute-done | bytes 131104 | tf_op jit(solution)/shard_map/ppermute | solution.py:32
  79.8 3.5 %collective-permute-start.21 = (bf16[64,256]{1,0:T(8,128)(2,1)S(1)}, bf16[64,256]{1,0:T(8,128)(2,1)S(1)}, u32[]{:S(2)}, u32[]{:S(2)}) collective-permute-start(bf16[64,256]{1,0:T(8,128)(2,1)S(1)} %get-tuple-element.42), channel_id=1, source_target_pairs={{0,64},{16,80},{32,96},{48,112},{64,0},{80,16},{96,32},{112,48},{1... | collective-permute-start | bytes 98312 | tf_op jit(solution)/shard_map/ppermute | solution.py:32
  85.5 2.9 %collective-permute-done.22 = bf16[64,256]{1,0:T(8,128)(2,1)S(1)} collective-permute-done((bf16[64,256]{1,0:T(8,128)(2,1)S(1)}, bf16[64,256]{1,0:T(8,128)(2,1)S(1)}, u32[]{:S(2)}, u32[]{:S(2)}) %collective-permute-start.22) | collective-permute-done | bytes 32800 | tf_op jit(solution)/shard_map/ppermute | solution.py:32
  89.6 2.7 %collective-permute-start.25 = (bf16[16,1280]{1,0:T(8,128)(2,1)S(1)}, bf16[16,1280]{1,0:T(8,128)(2,1)S(1)}, u32[]{:S(2)}, u32[]{:S(2)}) collective-permute-start(bf16[16,1280]{1,0:T(8,128)(2,1)S(1)} %get-tuple-element.31), channel_id=1, source_target_pairs={{0,9},{1,8},{2,11},{3,10},{4,13},{5,12},{6,15},{7,14},{8,1},{9,0},... | collective-permute-start | bytes 122888 | tf_op jit(solution)/shard_map/ppermute | solution.py:32
  94.5 3.4 %collective-permute-start.26 = (bf16[16,1280]{1,0:T(8,128)(2,1)S(1)}, bf16[16,1280]{1,0:T(8,128)(2,1)S(1)}, u32[]{:S(2)}, u32[]{:S(2)}) collective-permute-start(bf16[16,1280]{1,0:T(8,128)(2,1)S(1)} %fusion.33), channel_id=1, source_target_pairs={{0,2},{1,3},{2,0},{3,1},{4,6},{5,7},{6,4},{7,5},{8,10},{9,11},{10,... | collective-permute-start | bytes 122888 | tf_op jit(solution)/shard_map/ppermute | solution.py:32
  97.9 5.2 %collective-permute-start.27 = (bf16[16,1280]{1,0:T(8,128)(2,1)S(1)}, bf16[16,1280]{1,0:T(8,128)(2,1)S(1)}, u32[]{:S(2)}, u32[]{:S(2)}) collective-permute-start(bf16[16,1280]{1,0:T(8,128)(2,1)S(1)} %fusion.33), channel_id=1, source_target_pairs={{0,4},{1,5},{2,6},{3,7},{4,0},{5,1},{6,2},{7,3},{8,12},{9,13},{10,... | collective-permute-start | bytes 122888 | tf_op jit(solution)/shard_map/ppermute | solution.py:32
  103.1 2.7 %collective-permute-done.27 = bf16[16,1280]{1,0:T(8,128)(2,1)S(1)} collective-permute-done((bf16[16,1280]{1,0:T(8,128)(2,1)S(1)}, bf16[16,1280]{1,0:T(8,128)(2,1)S(1)}, u32[]{:S(2)}, u32[]{:S(2)}) %collective-permute-start.27) | collective-permute-done | bytes 40992 | tf_op jit(solution)/shard_map/ppermute | solution.py:32
  105.8 3.4 %collective-permute-done.28 = bf16[16,1280]{1,0:T(8,128)(2,1)S(1)} collective-permute-done((bf16[16,1280]{1,0:T(8,128)(2,1)S(1)}, bf16[16,1280]{1,0:T(8,128)(2,1)S(1)}, u32[]{:S(2)}, u32[]{:S(2)}) %collective-permute-start.28) | collective-permute-done | bytes 40992 | tf_op jit(solution)/shard_map/ppermute | solution.py:32
  110.4 2.0 %collective-permute-start.30 = (bf16[16,1280]{1,0:T(8,128)(2,1)S(1)}, bf16[16,1280]{1,0:T(8,128)(2,1)S(1)}, u32[]{:S(2)}, u32[]{:S(2)}) collective-permute-start(bf16[16,1280]{1,0:T(8,128)(2,1)S(1)} %fusion.54), channel_id=1, source_target_pairs={{0,8},{1,9},{2,10},{3,11},{4,12},{5,13},{6,14},{7,15},{8,0},{9,1},... | collective-permute-start | bytes 122888 | tf_op jit(solution)/shard_map/ppermute | solution.py:32
  114.4 2.9 %collective-permute-done.31 = bf16[16,1280]{1,0:T(8,128)(2,1)S(1)} collective-permute-done((bf16[16,1280]{1,0:T(8,128)(2,1)S(1)}, bf16[16,1280]{1,0:T(8,128)(2,1)S(1)}, u32[]{:S(2)}, u32[]{:S(2)}) %collective-permute-start.31) | collective-permute-done | bytes 40992 | tf_op jit(solution)/shard_map/ppermute | solution.py:32
  118.0 2.9 %fusion.76 = (bf16[64,1280]{1,0:T(8,128)(2,1)}, f32[64,1280]{1,0:T(8,128)}) fusion(bf16[1280,320]{0,1:T(8,128)(2,1)} %param.17, bf16[64,1280]{1,0:T(8,128)(2,1)} %bitcast.92, bf16[320,1280]{1,0:T(8,128)(2,1)S(1)} %copy-done, f32[64,320]{1,0:T(8,128)S(1)} %fusion.4), kind=kOutput, calls=%fused_computation.122 | convolution fusion | flops 105328640 | bytes 2375680 | tf_op jit(solution)/shard_map/dot_general | solution.py:62
  129.3 5.3 %all-to-all-start.1 = ((bf16[4,4,128,256]{3,2,1,0:T(8,128)(2,1)}), bf16[4,4,128,256]{3,2,1,0:T(8,128)(2,1)S(1)}, u32[]{:S(2)}, u32[]{:S(2)}) async-start(bf16[4,4,128,256]{3,2,1,0:T(8,128)(2,1)} %bitcast.90), calls=%async_computation.1 | async-start | bytes 2097152 | tf_op jit(solution)/shard_map/all_to_all | solution.py:28
  136.1 2.5 %collective-permute-start.36 = (bf16[16,1280]{1,0:T(8,128)(2,1)S(1)}, bf16[16,1280]{1,0:T(8,128)(2,1)S(1)}, u32[]{:S(2)}, u32[]{:S(2)}) collective-permute-start(bf16[16,1280]{1,0:T(8,128)(2,1)S(1)} %fusion.31), channel_id=1, source_target_pairs={{0,4},{1,5},{2,6},{3,7},{4,0},{5,1},{6,2},{7,3},{8,12},{9,13},{10,... | collective-permute-start | bytes 122888 | tf_op jit(solution)/shard_map/ppermute | solution.py:32
  138.6 3.5 %collective-permute-start.37 = (bf16[16,1280]{1,0:T(8,128)(2,1)S(1)}, bf16[16,1280]{1,0:T(8,128)(2,1)S(1)}, u32[]{:S(2)}, u32[]{:S(2)}) collective-permute-start(bf16[16,1280]{1,0:T(8,128)(2,1)S(1)} %fusion.31), channel_id=1, source_target_pairs={{0,6},{1,7},{2,4},{3,5},{4,2},{5,3},{6,0},{7,1},{8,14},{9,15},{10,... | collective-permute-start | bytes 122888 | tf_op jit(solution)/shard_map/ppermute | solution.py:32
  143.8 1.9 %collective-permute-done.36 = bf16[16,1280]{1,0:T(8,128)(2,1)S(1)} collective-permute-done((bf16[16,1280]{1,0:T(8,128)(2,1)S(1)}, bf16[16,1280]{1,0:T(8,128)(2,1)S(1)}, u32[]{:S(2)}, u32[]{:S(2)}) %collective-permute-start.36) | collective-permute-done | bytes 40992 | tf_op jit(solution)/shard_map/ppermute | solution.py:32
  146.2 2.2 %collective-permute-start.39 = (bf16[16,1280]{1,0:T(8,128)(2,1)S(1)}, bf16[16,1280]{1,0:T(8,128)(2,1)S(1)}, u32[]{:S(2)}, u32[]{:S(2)}) collective-permute-start(bf16[16,1280]{1,0:T(8,128)(2,1)S(1)} %add_convert_fusion.2), channel_id=1, source_target_pairs={{0,8},{1,9},{2,10},{3,11},{4,12},{5,13},{6,14},{7,15},{8,0},{9,1},... | collective-permute-start | bytes 122888 | tf_op jit(solution)/shard_map/ppermute | solution.py:32
  150.3 3.6 %collective-permute-done.40 = bf16[16,1280]{1,0:T(8,128)(2,1)S(1)} collective-permute-done((bf16[16,1280]{1,0:T(8,128)(2,1)S(1)}, bf16[16,1280]{1,0:T(8,128)(2,1)S(1)}, u32[]{:S(2)}, u32[]{:S(2)}) %collective-permute-start.40) | collective-permute-done | bytes 40992 | tf_op jit(solution)/shard_map/ppermute | solution.py:32
  154.4 5.8 %collective-permute-done.16 = bf16[2,128,256]{2,1,0:T(8,128)(2,1)S(1)} collective-permute-done((bf16[2,128,256]{2,1,0:T(8,128)(2,1)S(1)}, bf16[2,128,256]{2,1,0:T(8,128)(2,1)S(1)}, u32[]{:S(2)}, u32[]{:S(2)}) %collective-permute-start.16) | collective-permute-done | bytes 131104 | tf_op jit(solution)/shard_map/ppermute | solution.py:32
  160.2 3.2 %collective-permute-start.17 = (bf16[128,256]{1,0:T(8,128)(2,1)S(1)}, bf16[128,256]{1,0:T(8,128)(2,1)S(1)}, u32[]{:S(2)}, u32[]{:S(2)}) collective-permute-start(bf16[128,256]{1,0:T(8,128)(2,1)S(1)} %fusion.38), channel_id=1, source_target_pairs={{0,6},{1,7},{2,4},{3,5},{4,2},{5,3},{6,0},{7,1},{8,14},{9,15},{10,... | collective-permute-start | bytes 196616 | tf_op jit(solution)/shard_map/ppermute | solution.py:32
  164.2 2.5 %collective-permute-done.17 = bf16[128,256]{1,0:T(8,128)(2,1)S(1)} collective-permute-done((bf16[128,256]{1,0:T(8,128)(2,1)S(1)}, bf16[128,256]{1,0:T(8,128)(2,1)S(1)}, u32[]{:S(2)}, u32[]{:S(2)}) %collective-permute-start.17) | collective-permute-done | bytes 65568 | tf_op jit(solution)/shard_map/ppermute | solution.py:32
  (132 shorter events, 54.4 us)
Async XLA Ops:
  4.2 30.9 %all-to-all-start = ((bf16[4,1024,256]{2,1,0:T(8,128)(2,1)}), bf16[4,1024,256]{2,1,0:T(8,128)(2,1)S(1)}, u32[]{:S(2)}, u32[]{:S(2)}) async-start(bf16[4,1024,256]{2,1,0:T(8,128)(2,1)} %copy-done.1), calls=%async_computation | async-start | bytes 4194304 | tf_op jit(solution)/shard_map/all_to_all | solution.py:28
  14.7 4.9 %collective-permute-start.3 = (bf16[16,1280]{1,0:T(8,128)(2,1)S(1)}, bf16[16,1280]{1,0:T(8,128)(2,1)S(1)}, u32[]{:S(2)}, u32[]{:S(2)}) collective-permute-start(bf16[16,1280]{1,0:T(8,128)(2,1)S(1)} %get-tuple-element.34), channel_id=1, source_target_pairs={{0,9},{1,8},{2,11},{3,10},{4,13},{5,12},{6,15},{7,14},{8,1},{9,0},... | collective-permute-start | bytes 122888 | tf_op jit(solution)/shard_map/ppermute | solution.py:32
  19.6 16.7 %collective-permute-start.4 = (bf16[16,1280]{1,0:T(8,128)(2,1)S(1)}, bf16[16,1280]{1,0:T(8,128)(2,1)S(1)}, u32[]{:S(2)}, u32[]{:S(2)}) collective-permute-start(bf16[16,1280]{1,0:T(8,128)(2,1)S(1)} %fusion.35), channel_id=1, source_target_pairs={{0,2},{1,3},{2,0},{3,1},{4,6},{5,7},{6,4},{7,5},{8,10},{9,11},{10,... | collective-permute-start | bytes 122888 | tf_op jit(solution)/shard_map/ppermute | solution.py:32
  23.0 13.4 %collective-permute-start.5 = (bf16[16,1280]{1,0:T(8,128)(2,1)S(1)}, bf16[16,1280]{1,0:T(8,128)(2,1)S(1)}, u32[]{:S(2)}, u32[]{:S(2)}) collective-permute-start(bf16[16,1280]{1,0:T(8,128)(2,1)S(1)} %fusion.35), channel_id=1, source_target_pairs={{0,4},{1,5},{2,6},{3,7},{4,0},{5,1},{6,2},{7,3},{8,12},{9,13},{10,... | collective-permute-start | bytes 122888 | tf_op jit(solution)/shard_map/ppermute | solution.py:32
  28.4 8.0 %collective-permute-start.6 = (bf16[16,1280]{1,0:T(8,128)(2,1)S(1)}, bf16[16,1280]{1,0:T(8,128)(2,1)S(1)}, u32[]{:S(2)}, u32[]{:S(2)}) collective-permute-start(bf16[16,1280]{1,0:T(8,128)(2,1)S(1)} %fusion.35), channel_id=1, source_target_pairs={{0,6},{1,7},{2,4},{3,5},{4,2},{5,3},{6,0},{7,1},{8,14},{9,15},{10,... | collective-permute-start | bytes 122888 | tf_op jit(solution)/shard_map/ppermute | solution.py:32
  35.1 30.6 %collective-permute-start = (bf16[4,1024,256]{2,1,0:T(8,128)(2,1)S(1)}, bf16[4,1024,256]{2,1,0:T(8,128)(2,1)S(1)}, u32[]{:S(2)}, u32[]{:S(2)}) collective-permute-start(bf16[4,1024,256]{2,1,0:T(8,128)(2,1)S(1)} %all-to-all-done.own), channel_id=1, source_target_pairs={{0,16},{16,0},{32,48},{48,32},{64,80},{80,64},{96,112},{112,96},{1... | collective-permute-start | bytes 6291464 | tf_op jit(solution)/shard_map/ppermute | solution.py:32
  36.2 12.9 %collective-permute-start.10 = (bf16[2,1280,64]{1,2,0:T(8,128)(2,1)S(1)}, bf16[2,1280,64]{1,2,0:T(8,128)(2,1)S(1)}, u32[]{:S(2)}, u32[]{:S(2)}) collective-permute-start(bf16[2,1280,64]{1,2,0:T(8,128)(2,1)S(1)} %pad_maximum_fusion.1), channel_id=1, source_target_pairs={{0,1},{1,0},{2,3},{3,2},{4,5},{5,4},{6,7},{7,6},{8,9},{9,8},{10,11... | collective-permute-start | bytes 983048 | tf_op jit(solution)/shard_map/ppermute | solution.py:32
  37.3 10.4 %collective-permute-start.7 = (bf16[16,1280]{1,0:T(8,128)(2,1)S(1)}, bf16[16,1280]{1,0:T(8,128)(2,1)S(1)}, u32[]{:S(2)}, u32[]{:S(2)}) collective-permute-start(bf16[16,1280]{1,0:T(8,128)(2,1)S(1)} %fusion.37), channel_id=1, source_target_pairs={{0,1},{1,0},{2,3},{3,2},{4,5},{5,4},{6,7},{7,6},{8,9},{9,8},{10,11... | collective-permute-start | bytes 122888 | tf_op jit(solution)/shard_map/ppermute | solution.py:32
  39.3 8.4 %collective-permute-start.8 = (bf16[16,1280]{1,0:T(8,128)(2,1)S(1)}, bf16[16,1280]{1,0:T(8,128)(2,1)S(1)}, u32[]{:S(2)}, u32[]{:S(2)}) collective-permute-start(bf16[16,1280]{1,0:T(8,128)(2,1)S(1)} %fusion.37), channel_id=1, source_target_pairs={{0,8},{1,9},{2,10},{3,11},{4,12},{5,13},{6,14},{7,15},{8,0},{9,1},... | collective-permute-start | bytes 122888 | tf_op jit(solution)/shard_map/ppermute | solution.py:32
  40.8 8.3 %collective-permute-start.9 = (bf16[16,1280]{1,0:T(8,128)(2,1)S(1)}, bf16[16,1280]{1,0:T(8,128)(2,1)S(1)}, u32[]{:S(2)}, u32[]{:S(2)}) collective-permute-start(bf16[16,1280]{1,0:T(8,128)(2,1)S(1)} %fusion.37), channel_id=1, source_target_pairs={{0,9},{1,8},{2,11},{3,10},{4,13},{5,12},{6,15},{7,14},{8,1},{9,0},... | collective-permute-start | bytes 122888 | tf_op jit(solution)/shard_map/ppermute | solution.py:32
  50.4 5.5 %collective-permute-start.11 = (bf16[64,256]{1,0:T(8,128)(2,1)S(1)}, bf16[64,256]{1,0:T(8,128)(2,1)S(1)}, u32[]{:S(2)}, u32[]{:S(2)}) collective-permute-start(bf16[64,256]{1,0:T(8,128)(2,1)S(1)} %convolution_convert_fusion), channel_id=1, source_target_pairs={{0,128},{128,0},{1,129},{129,1},{2,130},{130,2},{3,131},{131,3},{4... | collective-permute-start | bytes 98312 | tf_op jit(solution)/shard_map/ppermute | solution.py:32
  56.6 5.8 %collective-permute-start.13 = (bf16[2,64,256]{2,1,0:T(8,128)(2,1)S(1)}, bf16[2,64,256]{2,1,0:T(8,128)(2,1)S(1)}, u32[]{:S(2)}, u32[]{:S(2)}) collective-permute-start(bf16[2,64,256]{2,1,0:T(8,128)(2,1)S(1)} %get-tuple-element.44), channel_id=1, source_target_pairs={{0,64},{16,80},{32,96},{48,112},{64,0},{80,16},{96,32},{112,48},{1... | collective-permute-start | bytes 196616 | tf_op jit(solution)/shard_map/ppermute | solution.py:32
  58.7 5.5 %collective-permute-start.14 = (bf16[2,64,256]{2,1,0:T(8,128)(2,1)S(1)}, bf16[2,64,256]{2,1,0:T(8,128)(2,1)S(1)}, u32[]{:S(2)}, u32[]{:S(2)}) collective-permute-start(bf16[2,64,256]{2,1,0:T(8,128)(2,1)S(1)} %get-tuple-element.44), channel_id=1, source_target_pairs={{0,96},{16,112},{32,64},{48,80},{64,32},{80,48},{96,0},{112,16},{1... | collective-permute-start | bytes 196616 | tf_op jit(solution)/shard_map/ppermute | solution.py:32
  64.2 5.1 %collective-permute-start.15 = (bf16[4,2,64,256]{3,2,1,0:T(8,128)(2,1)S(1)}, bf16[4,2,64,256]{3,2,1,0:T(8,128)(2,1)S(1)}, u32[]{:S(2)}, u32[]{:S(2)}) collective-permute-start(bf16[4,2,64,256]{3,2,1,0:T(8,128)(2,1)S(1)} %pad_maximum_fusion.2.own), channel_id=1, source_target_pairs={{0,16},{16,0},{32,48},{48,32},{64,80},{80,64},{96,112},{112,96},{1... | collective-permute-start | bytes 786440 | tf_op jit(solution)/shard_map/ppermute | solution.py:32
  72.2 7.4 %collective-permute-start.19 = (bf16[4,64,256]{2,1,0:T(8,128)(2,1)S(1)}, bf16[4,64,256]{2,1,0:T(8,128)(2,1)S(1)}, u32[]{:S(2)}, u32[]{:S(2)}) collective-permute-start(bf16[4,64,256]{2,1,0:T(8,128)(2,1)S(1)} %fusion.7), channel_id=1, source_target_pairs={{0,128},{128,0},{1,129},{129,1},{2,130},{130,2},{3,131},{131,3},{4... | collective-permute-start | bytes 393224 | tf_op jit(solution)/shard_map/ppermute | solution.py:32
  79.8 5.8 %collective-permute-start.21 = (bf16[64,256]{1,0:T(8,128)(2,1)S(1)}, bf16[64,256]{1,0:T(8,128)(2,1)S(1)}, u32[]{:S(2)}, u32[]{:S(2)}) collective-permute-start(bf16[64,256]{1,0:T(8,128)(2,1)S(1)} %get-tuple-element.42), channel_id=1, source_target_pairs={{0,64},{16,80},{32,96},{48,112},{64,0},{80,16},{96,32},{112,48},{1... | collective-permute-start | bytes 98312 | tf_op jit(solution)/shard_map/ppermute | solution.py:32
  83.3 5.1 %collective-permute-start.22 = (bf16[64,256]{1,0:T(8,128)(2,1)S(1)}, bf16[64,256]{1,0:T(8,128)(2,1)S(1)}, u32[]{:S(2)}, u32[]{:S(2)}) collective-permute-start(bf16[64,256]{1,0:T(8,128)(2,1)S(1)} %get-tuple-element.41), channel_id=1, source_target_pairs={{0,96},{16,112},{32,64},{48,80},{64,32},{80,48},{96,0},{112,16},{1... | collective-permute-start | bytes 98312 | tf_op jit(solution)/shard_map/ppermute | solution.py:32
  89.6 4.9 %collective-permute-start.25 = (bf16[16,1280]{1,0:T(8,128)(2,1)S(1)}, bf16[16,1280]{1,0:T(8,128)(2,1)S(1)}, u32[]{:S(2)}, u32[]{:S(2)}) collective-permute-start(bf16[16,1280]{1,0:T(8,128)(2,1)S(1)} %get-tuple-element.31), channel_id=1, source_target_pairs={{0,9},{1,8},{2,11},{3,10},{4,13},{5,12},{6,15},{7,14},{8,1},{9,0},... | collective-permute-start | bytes 122888 | tf_op jit(solution)/shard_map/ppermute | solution.py:32
  94.5 8.6 %collective-permute-start.26 = (bf16[16,1280]{1,0:T(8,128)(2,1)S(1)}, bf16[16,1280]{1,0:T(8,128)(2,1)S(1)}, u32[]{:S(2)}, u32[]{:S(2)}) collective-permute-start(bf16[16,1280]{1,0:T(8,128)(2,1)S(1)} %fusion.33), channel_id=1, source_target_pairs={{0,2},{1,3},{2,0},{3,1},{4,6},{5,7},{6,4},{7,5},{8,10},{9,11},{10,... | collective-permute-start | bytes 122888 | tf_op jit(solution)/shard_map/ppermute | solution.py:32
  97.9 7.9 %collective-permute-start.27 = (bf16[16,1280]{1,0:T(8,128)(2,1)S(1)}, bf16[16,1280]{1,0:T(8,128)(2,1)S(1)}, u32[]{:S(2)}, u32[]{:S(2)}) collective-permute-start(bf16[16,1280]{1,0:T(8,128)(2,1)S(1)} %fusion.33), channel_id=1, source_target_pairs={{0,4},{1,5},{2,6},{3,7},{4,0},{5,1},{6,2},{7,3},{8,12},{9,13},{10,... | collective-permute-start | bytes 122888 | tf_op jit(solution)/shard_map/ppermute | solution.py:32
  103.1 6.1 %collective-permute-start.28 = (bf16[16,1280]{1,0:T(8,128)(2,1)S(1)}, bf16[16,1280]{1,0:T(8,128)(2,1)S(1)}, u32[]{:S(2)}, u32[]{:S(2)}) collective-permute-start(bf16[16,1280]{1,0:T(8,128)(2,1)S(1)} %fusion.33), channel_id=1, source_target_pairs={{0,6},{1,7},{2,4},{3,5},{4,2},{5,3},{6,0},{7,1},{8,14},{9,15},{10,... | collective-permute-start | bytes 122888 | tf_op jit(solution)/shard_map/ppermute | solution.py:32
  112.4 5.0 %collective-permute-start.31 = (bf16[16,1280]{1,0:T(8,128)(2,1)S(1)}, bf16[16,1280]{1,0:T(8,128)(2,1)S(1)}, u32[]{:S(2)}, u32[]{:S(2)}) collective-permute-start(bf16[16,1280]{1,0:T(8,128)(2,1)S(1)} %fusion.54), channel_id=1, source_target_pairs={{0,9},{1,8},{2,11},{3,10},{4,13},{5,12},{6,15},{7,14},{8,1},{9,0},... | collective-permute-start | bytes 122888 | tf_op jit(solution)/shard_map/ppermute | solution.py:32
  122.3 12.3 %collective-permute-start.32 = (bf16[16,1280]{1,0:T(8,128)(2,1)}, bf16[16,1280]{1,0:T(8,128)(2,1)S(1)}, u32[]{:S(2)}, u32[]{:S(2)}) collective-permute-start(bf16[16,1280]{1,0:T(8,128)(2,1)} %get-tuple-element.27), channel_id=1, source_target_pairs={{0,1},{1,0},{2,3},{3,2},{4,5},{5,4},{6,7},{7,6},{8,9},{9,8},{10,11... | collective-permute-start | bytes 122888 | tf_op jit(solution)/shard_map/ppermute | solution.py:32
  124.1 10.6 %collective-permute-start.33 = (bf16[16,1280]{1,0:T(8,128)(2,1)}, bf16[16,1280]{1,0:T(8,128)(2,1)}, u32[]{:S(2)}, u32[]{:S(2)}) collective-permute-start(bf16[16,1280]{1,0:T(8,128)(2,1)} %get-tuple-element.29), channel_id=1, source_target_pairs={{0,8},{1,9},{2,10},{3,11},{4,12},{5,13},{6,14},{7,15},{8,0},{9,1},... | collective-permute-start | bytes 122888 | tf_op jit(solution)/shard_map/ppermute | solution.py:32
  124.1 10.6 %collective-permute-start.34 = (bf16[16,1280]{1,0:T(8,128)(2,1)S(1)}, bf16[16,1280]{1,0:T(8,128)(2,1)}, u32[]{:S(2)}, u32[]{:S(2)}) collective-permute-start(bf16[16,1280]{1,0:T(8,128)(2,1)S(1)} %get-tuple-element.28), channel_id=1, source_target_pairs={{0,9},{1,8},{2,11},{3,10},{4,13},{5,12},{6,15},{7,14},{8,1},{9,0},... | collective-permute-start | bytes 122888 | tf_op jit(solution)/shard_map/ppermute | solution.py:32
  129.3 24.7 %all-to-all-start.1 = ((bf16[4,4,128,256]{3,2,1,0:T(8,128)(2,1)}), bf16[4,4,128,256]{3,2,1,0:T(8,128)(2,1)S(1)}, u32[]{:S(2)}, u32[]{:S(2)}) async-start(bf16[4,4,128,256]{3,2,1,0:T(8,128)(2,1)} %bitcast.90), calls=%async_computation.1 | async-start | bytes 2097152 | tf_op jit(solution)/shard_map/all_to_all | solution.py:28
  135.6 8.2 %collective-permute-start.35 = (bf16[16,1280]{1,0:T(8,128)(2,1)S(1)}, bf16[16,1280]{1,0:T(8,128)(2,1)S(1)}, u32[]{:S(2)}, u32[]{:S(2)}) collective-permute-start(bf16[16,1280]{1,0:T(8,128)(2,1)S(1)} %fusion.31), channel_id=1, source_target_pairs={{0,2},{1,3},{2,0},{3,1},{4,6},{5,7},{6,4},{7,5},{8,10},{9,11},{10,... | collective-permute-start | bytes 122888 | tf_op jit(solution)/shard_map/ppermute | solution.py:32
  136.1 9.6 %collective-permute-start.36 = (bf16[16,1280]{1,0:T(8,128)(2,1)S(1)}, bf16[16,1280]{1,0:T(8,128)(2,1)S(1)}, u32[]{:S(2)}, u32[]{:S(2)}) collective-permute-start(bf16[16,1280]{1,0:T(8,128)(2,1)S(1)} %fusion.31), channel_id=1, source_target_pairs={{0,4},{1,5},{2,6},{3,7},{4,0},{5,1},{6,2},{7,3},{8,12},{9,13},{10,... | collective-permute-start | bytes 122888 | tf_op jit(solution)/shard_map/ppermute | solution.py:32
  138.6 7.1 %collective-permute-start.37 = (bf16[16,1280]{1,0:T(8,128)(2,1)S(1)}, bf16[16,1280]{1,0:T(8,128)(2,1)S(1)}, u32[]{:S(2)}, u32[]{:S(2)}) collective-permute-start(bf16[16,1280]{1,0:T(8,128)(2,1)S(1)} %fusion.31), channel_id=1, source_target_pairs={{0,6},{1,7},{2,4},{3,5},{4,2},{5,3},{6,0},{7,1},{8,14},{9,15},{10,... | collective-permute-start | bytes 122888 | tf_op jit(solution)/shard_map/ppermute | solution.py:32
  148.4 5.6 %collective-permute-start.40 = (bf16[16,1280]{1,0:T(8,128)(2,1)S(1)}, bf16[16,1280]{1,0:T(8,128)(2,1)S(1)}, u32[]{:S(2)}, u32[]{:S(2)}) collective-permute-start(bf16[16,1280]{1,0:T(8,128)(2,1)S(1)} %add_convert_fusion.2), channel_id=1, source_target_pairs={{0,9},{1,8},{2,11},{3,10},{4,13},{5,12},{6,15},{7,14},{8,1},{9,0},... | collective-permute-start | bytes 122888 | tf_op jit(solution)/shard_map/ppermute | solution.py:32
  154.1 6.1 %collective-permute-start.16 = (bf16[2,128,256]{2,1,0:T(8,128)(2,1)S(1)}, bf16[2,128,256]{2,1,0:T(8,128)(2,1)S(1)}, u32[]{:S(2)}, u32[]{:S(2)}) collective-permute-start(bf16[2,128,256]{2,1,0:T(8,128)(2,1)S(1)} %get-tuple-element.13), channel_id=1, source_target_pairs={{0,2},{1,3},{2,0},{3,1},{4,6},{5,7},{6,4},{7,5},{8,10},{9,11},{10,... | collective-permute-start | bytes 393224 | tf_op jit(solution)/shard_map/ppermute | solution.py:32
  160.2 6.5 %collective-permute-start.17 = (bf16[128,256]{1,0:T(8,128)(2,1)S(1)}, bf16[128,256]{1,0:T(8,128)(2,1)S(1)}, u32[]{:S(2)}, u32[]{:S(2)}) collective-permute-start(bf16[128,256]{1,0:T(8,128)(2,1)S(1)} %fusion.38), channel_id=1, source_target_pairs={{0,6},{1,7},{2,4},{3,5},{4,2},{5,3},{6,0},{7,1},{8,14},{9,15},{10,... | collective-permute-start | bytes 196616 | tf_op jit(solution)/shard_map/ppermute | solution.py:32
  (26 other events, 153.5 us)

commit v2 on v1

--- a/solution.py
+++ b/solution.py
@@ -42,13 +42,36 @@
     return (gelu_value, gelu_slope)
 
 
-def layer_norm(image_tokens, ln_gain, ln_bias):
-    image_float = image_tokens.astype(F32)
+def vision_kernel(*refs):
+    sources, outs, held, sems = refs[:5], refs[5:13], refs[13:18], refs[18]
+    own, one, two, three, image_own, hat_own, inv_own, slope = outs
+    image, gain, bias, mlp_in, mlp_out = held
+    copies = [pltpu.make_async_copy(source, target, sems.at[i]) for i, (source, target) in enumerate(zip(sources, held))]
+    for copy in copies:
+        copy.start()
+    m = lax.axis_index("mp")
+    near = (m & 1) | ((m >> 3) << 1)
+    rows = image.shape[0] // 4
+    copies[0].wait()
+    lines = [image[pl.ds(pl.multiple_of((near ^ k) * rows, rows), rows)] for k in range(4)]
+    image_float = jnp.concatenate([x.astype(F32) for x in lines], axis=0)
     centred = image_float - jnp.mean(image_float, axis=1, keepdims=True)
     inv_scale = lax.rsqrt(jnp.mean(centred * centred, axis=1, keepdims=True) + EPS_VISION)
     normed_hat = centred * inv_scale
-    normed = (normed_hat * ln_gain + ln_bias).astype(BF16)
-    return (image_float, normed_hat, inv_scale, normed)
+    copies[1].wait()
+    copies[2].wait()
+    normed = (normed_hat * gain[...][None, :] + bias[...][None, :]).astype(BF16)
+    copies[3].wait()
+    gelu_value, gelu_slope = gelu_parts(contract_last(normed, mlp_in[...]))
+    copies[4].wait()
+    term = jnp.dot(gelu_value.astype(BF16), mlp_out[...], preferred_element_type=F32)
+    own[...] = term[:rows]
+    for k, ref in enumerate((one, two, three)):
+        ref[...] = term[(k + 1) * rows : (k + 2) * rows].astype(BF16)
+    image_own[...] = image_float[:rows]
+    hat_own[...] = normed_hat[:rows]
+    inv_own[...] = jnp.broadcast_to(inv_scale[:rows], inv_own.shape)
+    slope[...] = gelu_slope
 
 
 def norm_backward(d_normed, normed_hat, inv_scale, ln_gain):
@@ -219,16 +242,20 @@
     along = exchanged(spread, "seq", ALONG_Y)
     weights = [along, swapped(along, "seq", 1)]
 
-    lines = image_tokens.reshape(4, chunk_rows, vision_width)
-    ordered = jnp.concatenate(
-        [lax.dynamic_slice_in_dim(lines, near_index ^ k, 1, 0) for k in range(4)], axis=0
-    ).reshape(image_rows, vision_width)
-    image_float, normed_hat, inv_scale, normed = layer_norm(ordered, ln_gain, ln_bias)
-    pre_act = jnp.dot(normed, mlp_in, preferred_element_type=F32)
-    gelu_value, gelu_slope = gelu_parts(pre_act)
-    mlp_term = jnp.dot(gelu_value.astype(BF16), mlp_out, preferred_element_type=F32)
-    mlp_chunk = reduced_chunk(mlp_term.reshape(4, chunk_rows, vision_width))
-    state_chunk = (image_float[:chunk_rows] + mlp_chunk).astype(BF16)
+    chunk = jax.ShapeDtypeStruct((chunk_rows, vision_width), F32)
+    sent = jax.ShapeDtypeStruct((chunk_rows, vision_width), BF16)
+    vision = (image_tokens, ln_gain, ln_bias, mlp_in.T, mlp_out)
+    *mlp_term, image_own, hat_own, inv_own, gelu_slope = pl.pallas_call(
+        vision_kernel,
+        out_shape=(chunk, sent, sent, sent, chunk, chunk)
+        + (jax.ShapeDtypeStruct((chunk_rows, HT), F32), jax.ShapeDtypeStruct((image_rows, mlp_in.shape[1]), F32)),
+        in_specs=[HBM] * len(vision),
+        out_specs=(VMEM,) * 8,
+        scratch_shapes=[pltpu.VMEM(x.shape, x.dtype) for x in vision] + [pltpu.SemaphoreType.DMA((len(vision),))],
+        compiler_params=SMALL_VMEM,
+        name="vision",
+    )(*[pltpu.with_memory_space_constraint(x, pltpu.HBM) for x in vision])
+    state_chunk = (image_own + reduced_chunk(mlp_term)).astype(BF16)
     image_state = gathered_chunks(state_chunk).reshape(image_rows, vision_width)
 
     partner_kv = swapped(jnp.stack([key_proj, value_proj]), "mp", 1)
@@ -279,7 +306,7 @@
     normed_term = contract_last(d_pre, mlp_in)
     d_normed = reduced_chunk(normed_term.reshape(4, chunk_rows, vision_width))
     grad_chunk = state_chunk_grad + norm_backward(
-        d_normed, normed_hat[:chunk_rows], inv_scale[:chunk_rows], ln_gain
+        d_normed, hat_own, inv_own[:, :1], ln_gain
     )
     grads = gathered_chunks(grad_chunk.astype(BF16))
     image_grad = jnp.concatenate(

time: 171 us -> 168 us (0.982)
  the two profiles are of different devices: /device:TPU:32 before, /device:TPU:4 now
where the time goes in v2:
time: 168 us
  waiting for transfers between devices  72.9 us (43%)
  starting transfers between devices  68.2 us (41%)
  local copies, waits for them, and re-layouts  8.12 us (5%)
  Pallas kernels  7.99 us (5%)
  other arithmetic  4.62 us (3%)
  matrix products  3.34 us (2%)
  between operations  2.37 us (1%)
    ppermute x41, waiting for transfers between devices, swapped(): lax.ppermute(x, axis, [(i, i ^ mask) for i in range(lax.axis_size(axis))])  64.9 us
    ppermute x41, starting transfers between devices, swapped(): lax.ppermute(x, axis, [(i, i ^ mask) for i in range(lax.axis_size(axis))])  60.1 us
    all_to_all x2, starting transfers between devices, exchanged(): return lax.all_to_all(x, axis, 0, 0, tiled=True, axis_index_groups=groups)  8.11 us
    all_to_all x2, waiting for transfers between devices, exchanged(): return lax.all_to_all(x, axis, 0, 0, tiled=True, axis_index_groups=groups)  8.05 us
    unnamed x30, local copies, waits for them, and re-layouts  6.48 us
    pallas_call x1, Pallas kernels, shards(): pl.pallas_call(text_kernel, out_shape=(small, small), in_specs=[SMEM] + [...  3.43 us
  transfers between devices with their start and end apart: 43, of which 28 were waited for; matrix products, arithmetic and copies ran while one was open for 2% of the time, Pallas kernels for 4%

profile of v2, /device:TPU:4, one launch (start us, length us, event | category | flops | bytes accessed | tf_op | source)
XLA Modules:
  0.0 167.5 jit_solution(11676516953202837862)
XLA Ops:
  4.1 4.5 %all-to-all-start = ((bf16[4,1024,256]{2,1,0:T(8,128)(2,1)}), bf16[4,1024,256]{2,1,0:T(8,128)(2,1)S(1)}, u32[]{:S(2)}, u32[]{:S(2)}) async-start(bf16[4,1024,256]{2,1,0:T(8,128)(2,1)} %copy-done), calls=%async_computation | async-start | bytes 4194304 | tf_op jit(solution)/shard_map/all_to_all | solution.py:28
  8.6 2.3 %vision.1 = (f32[16,1280]{1,0:T(8,128)S(1)}, bf16[16,1280]{1,0:T(8,128)(2,1)S(1)}, bf16[16,1280]{1,0:T(8,128)(2,1)S(1)}, bf16[16,1280]{1,0:T(8,128)(2,1)S(1)}, f...) custom-call(bf16[64,1280]{1,0:T(8,128)(2,1)} %refs_0_.1, ...), custom_call_target="tpu_custom_call" | custom-call | tf_op jit(solution)/shard_map/vision/pallas_call | solution.py:248
  15.0 2.4 %collective-permute-done.2 = bf16[16,1280]{1,0:T(8,128)(2,1)S(1)} collective-permute-done((bf16[16,1280]{1,0:T(8,128)(2,1)S(1)}, bf16[16,1280]{1,0:T(8,128)(2,1)S(1)}, u32[]{:S(2)}, u32[]{:S(2)}) %collective-permute-start.2) | collective-permute-done | bytes 40992 | tf_op jit(solution)/shard_map/ppermute | solution.py:32
  19.0 3.4 %collective-permute-start.4 = (bf16[16,1280]{1,0:T(8,128)(2,1)S(1)}, bf16[16,1280]{1,0:T(8,128)(2,1)S(1)}, u32[]{:S(2)}, u32[]{:S(2)}) collective-permute-start(bf16[16,1280]{1,0:T(8,128)(2,1)S(1)} %add_convert_fusion.2), channel_id=1, source_target_pairs={{0,2},{1,3},{2,0},{3,1},{4,6},{5,7},{6,4},{7,5},{8,10},{9,11},{10,... | collective-permute-start | bytes 122888 | tf_op jit(solution)/shard_map/ppermute | solution.py:32
  22.4 4.5 %collective-permute-start.5 = (bf16[16,1280]{1,0:T(8,128)(2,1)S(1)}, bf16[16,1280]{1,0:T(8,128)(2,1)S(1)}, u32[]{:S(2)}, u32[]{:S(2)}) collective-permute-start(bf16[16,1280]{1,0:T(8,128)(2,1)S(1)} %add_convert_fusion.2), channel_id=1, source_target_pairs={{0,4},{1,5},{2,6},{3,7},{4,0},{5,1},{6,2},{7,3},{8,12},{9,13},{10,... | collective-permute-start | bytes 122888 | tf_op jit(solution)/shard_map/ppermute | solution.py:32
  26.9 8.0 %all-to-all-done.own = bf16[4,1024,256]{2,1,0:T(8,128)(2,1)S(1)} async-done(((bf16[4,1024,256]{2,1,0:T(8,128)(2,1)}), bf16[4,1024,256]{2,1,0:T(8,128)(2,1)S(1)}, u32[]{:S(2)}, u32[]{:S(2)}) %all-to-all-start) | async-done | bytes 2097184 | tf_op jit(solution)/shard_map/all_to_all | solution.py:28
  39.8 2.2 %collective-permute-start.9 = (bf16[16,1280]{1,0:T(8,128)(2,1)S(1)}, bf16[16,1280]{1,0:T(8,128)(2,1)S(1)}, u32[]{:S(2)}, u32[]{:S(2)}) collective-permute-start(bf16[16,1280]{1,0:T(8,128)(2,1)S(1)} %add_convert_fusion.1), channel_id=1, source_target_pairs={{0,9},{1,8},{2,11},{3,10},{4,13},{5,12},{6,15},{7,14},{8,1},{9,0},... | collective-permute-start | bytes 122888 | tf_op jit(solution)/shard_map/ppermute | solution.py:32
  42.0 4.5 %collective-permute-done.7 = bf16[16,1280]{1,0:T(8,128)(2,1)S(1)} collective-permute-done((bf16[16,1280]{1,0:T(8,128)(2,1)S(1)}, bf16[16,1280]{1,0:T(8,128)(2,1)S(1)}, u32[]{:S(2)}, u32[]{:S(2)}) %collective-permute-start.7) | collective-permute-done | bytes 40992 | tf_op jit(solution)/shard_map/ppermute | solution.py:32
  49.0 4.6 %collective-permute-done.11 = bf16[64,256]{1,0:T(8,128)(2,1)S(1)} collective-permute-done((bf16[64,256]{1,0:T(8,128)(2,1)S(1)}, bf16[64,256]{1,0:T(8,128)(2,1)S(1)}, u32[]{:S(2)}, u32[]{:S(2)}) %collective-permute-start.11) | collective-permute-done | bytes 32800 | tf_op jit(solution)/shard_map/ppermute | solution.py:32
  54.3 2.1 %collective-permute-start.13 = (bf16[2,64,256]{2,1,0:T(8,128)(2,1)S(1)}, bf16[2,64,256]{2,1,0:T(8,128)(2,1)S(1)}, u32[]{:S(2)}, u32[]{:S(2)}) collective-permute-start(bf16[2,64,256]{2,1,0:T(8,128)(2,1)S(1)} %get-tuple-element.53), channel_id=1, source_target_pairs={{0,64},{16,80},{32,96},{48,112},{64,0},{80,16},{96,32},{112,48},{1... | collective-permute-start | bytes 196616 | tf_op jit(solution)/shard_map/ppermute | solution.py:32
  56.3 2.1 %collective-permute-start.14 = (bf16[2,64,256]{2,1,0:T(8,128)(2,1)S(1)}, bf16[2,64,256]{2,1,0:T(8,128)(2,1)S(1)}, u32[]{:S(2)}, u32[]{:S(2)}) collective-permute-start(bf16[2,64,256]{2,1,0:T(8,128)(2,1)S(1)} %get-tuple-element.53), channel_id=1, source_target_pairs={{0,96},{16,112},{32,64},{48,80},{64,32},{80,48},{96,0},{112,16},{1... | collective-permute-start | bytes 196616 | tf_op jit(solution)/shard_map/ppermute | solution.py:32
  63.5 3.4 %text_projections.1 = (bf16[128,256]{1,0:T(8,128)(2,1)S(1)}, bf16[128,256]{1,0:T(8,128)(2,1)S(1)}) custom-call(s32[1]{0:T(128)S(6)} %copy.17.doc, f32[1,1]{1,0:T(1,128)} %bitcast.75.gate, f32[1,4096]{1,0:T(1,128)S(1)} %bitcast.77, bf16[4,1024,256]{2,1,0:T(8,128)(2,1)S(1)} %all-to-all-done.own, bf16[4,1024,256]{2,1,0:T(8,128)(2,1)S(1)} %collective-permute-done.other, ...), custom_call_target="tpu_custom_call" | custom-call | tf_op jit(solution)/shard_map/text_projections/pallas_call | solution.py:271
  70.8 6.5 %collective-permute-done.19 = bf16[4,64,256]{2,1,0:T(8,128)(2,1)S(1)} collective-permute-done((bf16[4,64,256]{2,1,0:T(8,128)(2,1)S(1)}, bf16[4,64,256]{2,1,0:T(8,128)(2,1)S(1)}, u32[]{:S(2)}, u32[]{:S(2)}) %collective-permute-start.19) | collective-permute-done | bytes 131104 | tf_op jit(solution)/shard_map/ppermute | solution.py:32
  77.4 3.5 %collective-permute-start.21 = (bf16[64,256]{1,0:T(8,128)(2,1)S(1)}, bf16[64,256]{1,0:T(8,128)(2,1)S(1)}, u32[]{:S(2)}, u32[]{:S(2)}) collective-permute-start(bf16[64,256]{1,0:T(8,128)(2,1)S(1)} %get-tuple-element.51), channel_id=1, source_target_pairs={{0,64},{16,80},{32,96},{48,112},{64,0},{80,16},{96,32},{112,48},{1... | collective-permute-start | bytes 98312 | tf_op jit(solution)/shard_map/ppermute | solution.py:32
  83.2 2.9 %collective-permute-done.22 = bf16[64,256]{1,0:T(8,128)(2,1)S(1)} collective-permute-done((bf16[64,256]{1,0:T(8,128)(2,1)S(1)}, bf16[64,256]{1,0:T(8,128)(2,1)S(1)}, u32[]{:S(2)}, u32[]{:S(2)}) %collective-permute-start.22) | collective-permute-done | bytes 32800 | tf_op jit(solution)/shard_map/ppermute | solution.py:32
  93.9 3.4 %collective-permute-start.26 = (bf16[16,1280]{1,0:T(8,128)(2,1)S(1)}, bf16[16,1280]{1,0:T(8,128)(2,1)S(1)}, u32[]{:S(2)}, u32[]{:S(2)}) collective-permute-start(bf16[16,1280]{1,0:T(8,128)(2,1)S(1)} %fusion.14), channel_id=1, source_target_pairs={{0,2},{1,3},{2,0},{3,1},{4,6},{5,7},{6,4},{7,5},{8,10},{9,11},{10,... | collective-permute-start | bytes 122888 | tf_op jit(solution)/shard_map/ppermute | solution.py:32
  97.3 4.6 %collective-permute-start.27 = (bf16[16,1280]{1,0:T(8,128)(2,1)S(1)}, bf16[16,1280]{1,0:T(8,128)(2,1)S(1)}, u32[]{:S(2)}, u32[]{:S(2)}) collective-permute-start(bf16[16,1280]{1,0:T(8,128)(2,1)S(1)} %fusion.14), channel_id=1, source_target_pairs={{0,4},{1,5},{2,6},{3,7},{4,0},{5,1},{6,2},{7,3},{8,12},{9,13},{10,... | collective-permute-start | bytes 122888 | tf_op jit(solution)/shard_map/ppermute | solution.py:32
  101.9 3.3 %collective-permute-done.27 = bf16[16,1280]{1,0:T(8,128)(2,1)S(1)} collective-permute-done((bf16[16,1280]{1,0:T(8,128)(2,1)S(1)}, bf16[16,1280]{1,0:T(8,128)(2,1)S(1)}, u32[]{:S(2)}, u32[]{:S(2)}) %collective-permute-start.27) | collective-permute-done | bytes 40992 | tf_op jit(solution)/shard_map/ppermute | solution.py:32
  105.2 2.8 %collective-permute-done.28 = bf16[16,1280]{1,0:T(8,128)(2,1)S(1)} collective-permute-done((bf16[16,1280]{1,0:T(8,128)(2,1)S(1)}, bf16[16,1280]{1,0:T(8,128)(2,1)S(1)}, u32[]{:S(2)}, u32[]{:S(2)}) %collective-permute-start.28) | collective-permute-done | bytes 40992 | tf_op jit(solution)/shard_map/ppermute | solution.py:32
  109.0 2.4 %collective-permute-start.30 = (bf16[16,1280]{1,0:T(8,128)(2,1)S(1)}, bf16[16,1280]{1,0:T(8,128)(2,1)S(1)}, u32[]{:S(2)}, u32[]{:S(2)}) collective-permute-start(bf16[16,1280]{1,0:T(8,128)(2,1)S(1)} %fusion.20), channel_id=1, source_target_pairs={{0,8},{1,9},{2,10},{3,11},{4,12},{5,13},{6,14},{7,15},{8,0},{9,1},... | collective-permute-start | bytes 122888 | tf_op jit(solution)/shard_map/ppermute | solution.py:32
  113.4 3.0 %collective-permute-done.31 = bf16[16,1280]{1,0:T(8,128)(2,1)S(1)} collective-permute-done((bf16[16,1280]{1,0:T(8,128)(2,1)S(1)}, bf16[16,1280]{1,0:T(8,128)(2,1)S(1)}, u32[]{:S(2)}, u32[]{:S(2)}) %collective-permute-start.31) | collective-permute-done | bytes 40992 | tf_op jit(solution)/shard_map/ppermute | solution.py:32
  116.5 2.8 %fusion.30 = (bf16[64,1280]{1,0:T(8,128)(2,1)}, f32[64,1280]{1,0:T(8,128)}) fusion(bf16[1280,320]{0,1:T(8,128)(2,1)S(1)} %copy-done.7, f32[64,320]{1,0:T(8,128)S(1)} %get-tuple-element.30, bf16[64,1280]{1,0:T(8,128)(2,1)S(1)} %bitcast.79, bf16[320,1280]{1,0:T(8,128)(2,1)} %refs_4_.1), kind=kOutput, calls=%fused_computation.65 | convolution fusion | flops 104980480 | bytes 2375680 | tf_op jit(solution)/shard_map/dot_general | solution.py:85
  121.4 2.9 %collective-permute-start.34 = (bf16[16,1280]{1,0:T(8,128)(2,1)S(1)}, bf16[16,1280]{1,0:T(8,128)(2,1)}, u32[]{:S(2)}, u32[]{:S(2)}) collective-permute-start(bf16[16,1280]{1,0:T(8,128)(2,1)S(1)} %get-tuple-element.44), channel_id=1, source_target_pairs={{0,9},{1,8},{2,11},{3,10},{4,13},{5,12},{6,15},{7,14},{8,1},{9,0},... | collective-permute-start | bytes 122888 | tf_op jit(solution)/shard_map/ppermute | solution.py:32
  127.7 3.6 %all-to-all-start.1 = ((bf16[4,4,128,256]{3,2,1,0:T(8,128)(2,1)}), bf16[4,4,128,256]{3,2,1,0:T(8,128)(2,1)S(1)}, u32[]{:S(2)}, u32[]{:S(2)}) async-start(bf16[4,4,128,256]{3,2,1,0:T(8,128)(2,1)} %bitcast.76), calls=%async_computation.1 | async-start | bytes 2097152 | tf_op jit(solution)/shard_map/all_to_all | solution.py:28
  133.0 2.8 %collective-permute-start.36 = (bf16[16,1280]{1,0:T(8,128)(2,1)S(1)}, bf16[16,1280]{1,0:T(8,128)(2,1)S(1)}, u32[]{:S(2)}, u32[]{:S(2)}) collective-permute-start(bf16[16,1280]{1,0:T(8,128)(2,1)S(1)} %fusion.12), channel_id=1, source_target_pairs={{0,4},{1,5},{2,6},{3,7},{4,0},{5,1},{6,2},{7,3},{8,12},{9,13},{10,... | collective-permute-start | bytes 122888 | tf_op jit(solution)/shard_map/ppermute | solution.py:32
  135.8 3.1 %collective-permute-start.37 = (bf16[16,1280]{1,0:T(8,128)(2,1)S(1)}, bf16[16,1280]{1,0:T(8,128)(2,1)S(1)}, u32[]{:S(2)}, u32[]{:S(2)}) collective-permute-start(bf16[16,1280]{1,0:T(8,128)(2,1)S(1)} %fusion.12), channel_id=1, source_target_pairs={{0,6},{1,7},{2,4},{3,5},{4,2},{5,3},{6,0},{7,1},{8,14},{9,15},{10,... | collective-permute-start | bytes 122888 | tf_op jit(solution)/shard_map/ppermute | solution.py:32
  139.6 3.2 %collective-permute-done.36 = bf16[16,1280]{1,0:T(8,128)(2,1)S(1)} collective-permute-done((bf16[16,1280]{1,0:T(8,128)(2,1)S(1)}, bf16[16,1280]{1,0:T(8,128)(2,1)S(1)}, u32[]{:S(2)}, u32[]{:S(2)}) %collective-permute-start.36) | collective-permute-done | bytes 40992 | tf_op jit(solution)/shard_map/ppermute | solution.py:32
  143.1 2.1 %collective-permute-start.38 = (bf16[16,1280]{1,0:T(8,128)(2,1)S(1)}, bf16[16,1280]{1,0:T(8,128)(2,1)S(1)}, u32[]{:S(2)}, u32[]{:S(2)}) collective-permute-start(bf16[16,1280]{1,0:T(8,128)(2,1)S(1)} %add_convert_fusion), channel_id=1, source_target_pairs={{0,1},{1,0},{2,3},{3,2},{4,5},{5,4},{6,7},{7,6},{8,9},{9,8},{10,11... | collective-permute-start | bytes 122888 | tf_op jit(solution)/shard_map/ppermute | solution.py:32
  147.2 2.0 %collective-permute-done.39 = bf16[16,1280]{1,0:T(8,128)(2,1)S(1)} collective-permute-done((bf16[16,1280]{1,0:T(8,128)(2,1)S(1)}, bf16[16,1280]{1,0:T(8,128)(2,1)S(1)}, u32[]{:S(2)}, u32[]{:S(2)}) %collective-permute-start.39) | collective-permute-done | bytes 40992 | tf_op jit(solution)/shard_map/ppermute | solution.py:32
  149.2 2.8 %collective-permute-done.40 = bf16[16,1280]{1,0:T(8,128)(2,1)S(1)} collective-permute-done((bf16[16,1280]{1,0:T(8,128)(2,1)S(1)}, bf16[16,1280]{1,0:T(8,128)(2,1)S(1)}, u32[]{:S(2)}, u32[]{:S(2)}) %collective-permute-start.40) | collective-permute-done | bytes 40992 | tf_op jit(solution)/shard_map/ppermute | solution.py:32
  153.2 6.3 %collective-permute-done.16 = bf16[2,128,256]{2,1,0:T(8,128)(2,1)S(1)} collective-permute-done((bf16[2,128,256]{2,1,0:T(8,128)(2,1)S(1)}, bf16[2,128,256]{2,1,0:T(8,128)(2,1)S(1)}, u32[]{:S(2)}, u32[]{:S(2)}) %collective-permute-start.16) | collective-permute-done | bytes 131104 | tf_op jit(solution)/shard_map/ppermute | solution.py:32
  161.3 4.7 %collective-permute-done.17 = bf16[128,256]{1,0:T(8,128)(2,1)S(1)} collective-permute-done((bf16[128,256]{1,0:T(8,128)(2,1)S(1)}, bf16[128,256]{1,0:T(8,128)(2,1)S(1)}, u32[]{:S(2)}, u32[]{:S(2)}) %collective-permute-start.17) | collective-permute-done | bytes 65568 | tf_op jit(solution)/shard_map/ppermute | solution.py:32
  (121 shorter events, 52.5 us)
Async XLA Ops:
  4.1 30.8 %all-to-all-start = ((bf16[4,1024,256]{2,1,0:T(8,128)(2,1)}), bf16[4,1024,256]{2,1,0:T(8,128)(2,1)S(1)}, u32[]{:S(2)}, u32[]{:S(2)}) async-start(bf16[4,1024,256]{2,1,0:T(8,128)(2,1)} %copy-done), calls=%async_computation | async-start | bytes 4194304 | tf_op jit(solution)/shard_map/all_to_all | solution.py:28
  14.1 4.9 %collective-permute-start.3 = (bf16[16,1280]{1,0:T(8,128)(2,1)S(1)}, bf16[16,1280]{1,0:T(8,128)(2,1)S(1)}, u32[]{:S(2)}, u32[]{:S(2)}) collective-permute-start(bf16[16,1280]{1,0:T(8,128)(2,1)S(1)} %get-tuple-element.23), channel_id=1, source_target_pairs={{0,9},{1,8},{2,11},{3,10},{4,13},{5,12},{6,15},{7,14},{8,1},{9,0},... | collective-permute-start | bytes 122888 | tf_op jit(solution)/shard_map/ppermute | solution.py:32
  19.0 18.0 %collective-permute-start.4 = (bf16[16,1280]{1,0:T(8,128)(2,1)S(1)}, bf16[16,1280]{1,0:T(8,128)(2,1)S(1)}, u32[]{:S(2)}, u32[]{:S(2)}) collective-permute-start(bf16[16,1280]{1,0:T(8,128)(2,1)S(1)} %add_convert_fusion.2), channel_id=1, source_target_pairs={{0,2},{1,3},{2,0},{3,1},{4,6},{5,7},{6,4},{7,5},{8,10},{9,11},{10,... | collective-permute-start | bytes 122888 | tf_op jit(solution)/shard_map/ppermute | solution.py:32
  22.4 14.6 %collective-permute-start.5 = (bf16[16,1280]{1,0:T(8,128)(2,1)S(1)}, bf16[16,1280]{1,0:T(8,128)(2,1)S(1)}, u32[]{:S(2)}, u32[]{:S(2)}) collective-permute-start(bf16[16,1280]{1,0:T(8,128)(2,1)S(1)} %add_convert_fusion.2), channel_id=1, source_target_pairs={{0,4},{1,5},{2,6},{3,7},{4,0},{5,1},{6,2},{7,3},{8,12},{9,13},{10,... | collective-permute-start | bytes 122888 | tf_op jit(solution)/shard_map/ppermute | solution.py:32
  26.9 10.1 %collective-permute-start.6 = (bf16[16,1280]{1,0:T(8,128)(2,1)S(1)}, bf16[16,1280]{1,0:T(8,128)(2,1)S(1)}, u32[]{:S(2)}, u32[]{:S(2)}) collective-permute-start(bf16[16,1280]{1,0:T(8,128)(2,1)S(1)} %add_convert_fusion.2), channel_id=1, source_target_pairs={{0,6},{1,7},{2,4},{3,5},{4,2},{5,3},{6,0},{7,1},{8,14},{9,15},{10,... | collective-permute-start | bytes 122888 | tf_op jit(solution)/shard_map/ppermute | solution.py:32
  34.9 28.5 %collective-permute-start = (bf16[4,1024,256]{2,1,0:T(8,128)(2,1)S(1)}, bf16[4,1024,256]{2,1,0:T(8,128)(2,1)S(1)}, u32[]{:S(2)}, u32[]{:S(2)}) collective-permute-start(bf16[4,1024,256]{2,1,0:T(8,128)(2,1)S(1)} %all-to-all-done.own), channel_id=1, source_target_pairs={{0,16},{16,0},{32,48},{48,32},{64,80},{80,64},{96,112},{112,96},{1... | collective-permute-start | bytes 6291464 | tf_op jit(solution)/shard_map/ppermute | solution.py:32
  35.0 12.8 %collective-permute-start.10 = (bf16[2,1280,64]{1,2,0:T(8,128)(2,1)S(1)}, bf16[2,1280,64]{1,2,0:T(8,128)(2,1)S(1)}, u32[]{:S(2)}, u32[]{:S(2)}) collective-permute-start(bf16[2,1280,64]{1,2,0:T(8,128)(2,1)S(1)} %pad_maximum_fusion.1), channel_id=1, source_target_pairs={{0,1},{1,0},{2,3},{3,2},{4,5},{5,4},{6,7},{7,6},{8,9},{9,8},{10,11... | collective-permute-start | bytes 983048 | tf_op jit(solution)/shard_map/ppermute | solution.py:32
  38.4 8.1 %collective-permute-start.7 = (bf16[16,1280]{1,0:T(8,128)(2,1)S(1)}, bf16[16,1280]{1,0:T(8,128)(2,1)S(1)}, u32[]{:S(2)}, u32[]{:S(2)}) collective-permute-start(bf16[16,1280]{1,0:T(8,128)(2,1)S(1)} %add_convert_fusion.1), channel_id=1, source_target_pairs={{0,1},{1,0},{2,3},{3,2},{4,5},{5,4},{6,7},{7,6},{8,9},{9,8},{10,11... | collective-permute-start | bytes 122888 | tf_op jit(solution)/shard_map/ppermute | solution.py:32
  38.6 7.9 %collective-permute-start.8 = (bf16[16,1280]{1,0:T(8,128)(2,1)S(1)}, bf16[16,1280]{1,0:T(8,128)(2,1)S(1)}, u32[]{:S(2)}, u32[]{:S(2)}) collective-permute-start(bf16[16,1280]{1,0:T(8,128)(2,1)S(1)} %add_convert_fusion.1), channel_id=1, source_target_pairs={{0,8},{1,9},{2,10},{3,11},{4,12},{5,13},{6,14},{7,15},{8,0},{9,1},... | collective-permute-start | bytes 122888 | tf_op jit(solution)/shard_map/ppermute | solution.py:32
  39.8 7.9 %collective-permute-start.9 = (bf16[16,1280]{1,0:T(8,128)(2,1)S(1)}, bf16[16,1280]{1,0:T(8,128)(2,1)S(1)}, u32[]{:S(2)}, u32[]{:S(2)}) collective-permute-start(bf16[16,1280]{1,0:T(8,128)(2,1)S(1)} %add_convert_fusion.1), channel_id=1, source_target_pairs={{0,9},{1,8},{2,11},{3,10},{4,13},{5,12},{6,15},{7,14},{8,1},{9,0},... | collective-permute-start | bytes 122888 | tf_op jit(solution)/shard_map/ppermute | solution.py:32
  48.1 5.5 %collective-permute-start.11 = (bf16[64,256]{1,0:T(8,128)(2,1)S(1)}, bf16[64,256]{1,0:T(8,128)(2,1)S(1)}, u32[]{:S(2)}, u32[]{:S(2)}) collective-permute-start(bf16[64,256]{1,0:T(8,128)(2,1)S(1)} %convolution_convert_fusion), channel_id=1, source_target_pairs={{0,128},{128,0},{1,129},{129,1},{2,130},{130,2},{3,131},{131,3},{4... | collective-permute-start | bytes 98312 | tf_op jit(solution)/shard_map/ppermute | solution.py:32
  54.3 5.8 %collective-permute-start.13 = (bf16[2,64,256]{2,1,0:T(8,128)(2,1)S(1)}, bf16[2,64,256]{2,1,0:T(8,128)(2,1)S(1)}, u32[]{:S(2)}, u32[]{:S(2)}) collective-permute-start(bf16[2,64,256]{2,1,0:T(8,128)(2,1)S(1)} %get-tuple-element.53), channel_id=1, source_target_pairs={{0,64},{16,80},{32,96},{48,112},{64,0},{80,16},{96,32},{112,48},{1... | collective-permute-start | bytes 196616 | tf_op jit(solution)/shard_map/ppermute | solution.py:32
  56.3 5.5 %collective-permute-start.14 = (bf16[2,64,256]{2,1,0:T(8,128)(2,1)S(1)}, bf16[2,64,256]{2,1,0:T(8,128)(2,1)S(1)}, u32[]{:S(2)}, u32[]{:S(2)}) collective-permute-start(bf16[2,64,256]{2,1,0:T(8,128)(2,1)S(1)} %get-tuple-element.53), channel_id=1, source_target_pairs={{0,96},{16,112},{32,64},{48,80},{64,32},{80,48},{96,0},{112,16},{1... | collective-permute-start | bytes 196616 | tf_op jit(solution)/shard_map/ppermute | solution.py:32
  61.9 5.1 %collective-permute-start.15 = (bf16[4,2,64,256]{3,2,1,0:T(8,128)(2,1)S(1)}, bf16[4,2,64,256]{3,2,1,0:T(8,128)(2,1)S(1)}, u32[]{:S(2)}, u32[]{:S(2)}) collective-permute-start(bf16[4,2,64,256]{3,2,1,0:T(8,128)(2,1)S(1)} %pad_maximum_fusion.2.own), channel_id=1, source_target_pairs={{0,16},{16,0},{32,48},{48,32},{64,80},{80,64},{96,112},{112,96},{1... | collective-permute-start | bytes 786440 | tf_op jit(solution)/shard_map/ppermute | solution.py:32
  69.9 7.4 %collective-permute-start.19 = (bf16[4,64,256]{2,1,0:T(8,128)(2,1)S(1)}, bf16[4,64,256]{2,1,0:T(8,128)(2,1)S(1)}, u32[]{:S(2)}, u32[]{:S(2)}) collective-permute-start(bf16[4,64,256]{2,1,0:T(8,128)(2,1)S(1)} %fusion.3), channel_id=1, source_target_pairs={{0,128},{128,0},{1,129},{129,1},{2,130},{130,2},{3,131},{131,3},{4... | collective-permute-start | bytes 393224 | tf_op jit(solution)/shard_map/ppermute | solution.py:32
  77.4 5.8 %collective-permute-start.21 = (bf16[64,256]{1,0:T(8,128)(2,1)S(1)}, bf16[64,256]{1,0:T(8,128)(2,1)S(1)}, u32[]{:S(2)}, u32[]{:S(2)}) collective-permute-start(bf16[64,256]{1,0:T(8,128)(2,1)S(1)} %get-tuple-element.51), channel_id=1, source_target_pairs={{0,64},{16,80},{32,96},{48,112},{64,0},{80,16},{96,32},{112,48},{1... | collective-permute-start | bytes 98312 | tf_op jit(solution)/shard_map/ppermute | solution.py:32
  80.9 5.1 %collective-permute-start.22 = (bf16[64,256]{1,0:T(8,128)(2,1)S(1)}, bf16[64,256]{1,0:T(8,128)(2,1)S(1)}, u32[]{:S(2)}, u32[]{:S(2)}) collective-permute-start(bf16[64,256]{1,0:T(8,128)(2,1)S(1)} %get-tuple-element.50), channel_id=1, source_target_pairs={{0,96},{16,112},{32,64},{48,80},{64,32},{80,48},{96,0},{112,16},{1... | collective-permute-start | bytes 98312 | tf_op jit(solution)/shard_map/ppermute | solution.py:32
  89.0 4.9 %collective-permute-start.25 = (bf16[16,1280]{1,0:T(8,128)(2,1)S(1)}, bf16[16,1280]{1,0:T(8,128)(2,1)S(1)}, u32[]{:S(2)}, u32[]{:S(2)}) collective-permute-start(bf16[16,1280]{1,0:T(8,128)(2,1)S(1)} %get-tuple-element.47), channel_id=1, source_target_pairs={{0,9},{1,8},{2,11},{3,10},{4,13},{5,12},{6,15},{7,14},{8,1},{9,0},... | collective-permute-start | bytes 122888 | tf_op jit(solution)/shard_map/ppermute | solution.py:32
  93.9 8.0 %collective-permute-start.26 = (bf16[16,1280]{1,0:T(8,128)(2,1)S(1)}, bf16[16,1280]{1,0:T(8,128)(2,1)S(1)}, u32[]{:S(2)}, u32[]{:S(2)}) collective-permute-start(bf16[16,1280]{1,0:T(8,128)(2,1)S(1)} %fusion.14), channel_id=1, source_target_pairs={{0,2},{1,3},{2,0},{3,1},{4,6},{5,7},{6,4},{7,5},{8,10},{9,11},{10,... | collective-permute-start | bytes 122888 | tf_op jit(solution)/shard_map/ppermute | solution.py:32
  97.3 7.9 %collective-permute-start.27 = (bf16[16,1280]{1,0:T(8,128)(2,1)S(1)}, bf16[16,1280]{1,0:T(8,128)(2,1)S(1)}, u32[]{:S(2)}, u32[]{:S(2)}) collective-permute-start(bf16[16,1280]{1,0:T(8,128)(2,1)S(1)} %fusion.14), channel_id=1, source_target_pairs={{0,4},{1,5},{2,6},{3,7},{4,0},{5,1},{6,2},{7,3},{8,12},{9,13},{10,... | collective-permute-start | bytes 122888 | tf_op jit(solution)/shard_map/ppermute | solution.py:32
  101.9 6.1 %collective-permute-start.28 = (bf16[16,1280]{1,0:T(8,128)(2,1)S(1)}, bf16[16,1280]{1,0:T(8,128)(2,1)S(1)}, u32[]{:S(2)}, u32[]{:S(2)}) collective-permute-start(bf16[16,1280]{1,0:T(8,128)(2,1)S(1)} %fusion.14), channel_id=1, source_target_pairs={{0,6},{1,7},{2,4},{3,5},{4,2},{5,3},{6,0},{7,1},{8,14},{9,15},{10,... | collective-permute-start | bytes 122888 | tf_op jit(solution)/shard_map/ppermute | solution.py:32
  111.5 5.0 %collective-permute-start.31 = (bf16[16,1280]{1,0:T(8,128)(2,1)S(1)}, bf16[16,1280]{1,0:T(8,128)(2,1)S(1)}, u32[]{:S(2)}, u32[]{:S(2)}) collective-permute-start(bf16[16,1280]{1,0:T(8,128)(2,1)S(1)} %fusion.20), channel_id=1, source_target_pairs={{0,9},{1,8},{2,11},{3,10},{4,13},{5,12},{6,15},{7,14},{8,1},{9,0},... | collective-permute-start | bytes 122888 | tf_op jit(solution)/shard_map/ppermute | solution.py:32
  120.7 10.6 %collective-permute-start.32 = (bf16[16,1280]{1,0:T(8,128)(2,1)}, bf16[16,1280]{1,0:T(8,128)(2,1)S(1)}, u32[]{:S(2)}, u32[]{:S(2)}) collective-permute-start(bf16[16,1280]{1,0:T(8,128)(2,1)} %get-tuple-element.43), channel_id=1, source_target_pairs={{0,1},{1,0},{2,3},{3,2},{4,5},{5,4},{6,7},{7,6},{8,9},{9,8},{10,11... | collective-permute-start | bytes 122888 | tf_op jit(solution)/shard_map/ppermute | solution.py:32
  121.4 10.0 %collective-permute-start.33 = (bf16[16,1280]{1,0:T(8,128)(2,1)}, bf16[16,1280]{1,0:T(8,128)(2,1)}, u32[]{:S(2)}, u32[]{:S(2)}) collective-permute-start(bf16[16,1280]{1,0:T(8,128)(2,1)} %get-tuple-element.45), channel_id=1, source_target_pairs={{0,8},{1,9},{2,10},{3,11},{4,12},{5,13},{6,14},{7,15},{8,0},{9,1},... | collective-permute-start | bytes 122888 | tf_op jit(solution)/shard_map/ppermute | solution.py:32
  121.4 10.0 %collective-permute-start.34 = (bf16[16,1280]{1,0:T(8,128)(2,1)S(1)}, bf16[16,1280]{1,0:T(8,128)(2,1)}, u32[]{:S(2)}, u32[]{:S(2)}) collective-permute-start(bf16[16,1280]{1,0:T(8,128)(2,1)S(1)} %get-tuple-element.44), channel_id=1, source_target_pairs={{0,9},{1,8},{2,11},{3,10},{4,13},{5,12},{6,15},{7,14},{8,1},{9,0},... | collective-permute-start | bytes 122888 | tf_op jit(solution)/shard_map/ppermute | solution.py:32
  127.7 24.4 %all-to-all-start.1 = ((bf16[4,4,128,256]{3,2,1,0:T(8,128)(2,1)}), bf16[4,4,128,256]{3,2,1,0:T(8,128)(2,1)S(1)}, u32[]{:S(2)}, u32[]{:S(2)}) async-start(bf16[4,4,128,256]{3,2,1,0:T(8,128)(2,1)} %bitcast.76), calls=%async_computation.1 | async-start | bytes 2097152 | tf_op jit(solution)/shard_map/all_to_all | solution.py:28
  132.3 7.3 %collective-permute-start.35 = (bf16[16,1280]{1,0:T(8,128)(2,1)S(1)}, bf16[16,1280]{1,0:T(8,128)(2,1)S(1)}, u32[]{:S(2)}, u32[]{:S(2)}) collective-permute-start(bf16[16,1280]{1,0:T(8,128)(2,1)S(1)} %fusion.12), channel_id=1, source_target_pairs={{0,2},{1,3},{2,0},{3,1},{4,6},{5,7},{6,4},{7,5},{8,10},{9,11},{10,... | collective-permute-start | bytes 122888 | tf_op jit(solution)/shard_map/ppermute | solution.py:32
  133.0 9.8 %collective-permute-start.36 = (bf16[16,1280]{1,0:T(8,128)(2,1)S(1)}, bf16[16,1280]{1,0:T(8,128)(2,1)S(1)}, u32[]{:S(2)}, u32[]{:S(2)}) collective-permute-start(bf16[16,1280]{1,0:T(8,128)(2,1)S(1)} %fusion.12), channel_id=1, source_target_pairs={{0,4},{1,5},{2,6},{3,7},{4,0},{5,1},{6,2},{7,3},{8,12},{9,13},{10,... | collective-permute-start | bytes 122888 | tf_op jit(solution)/shard_map/ppermute | solution.py:32
  135.8 7.0 %collective-permute-start.37 = (bf16[16,1280]{1,0:T(8,128)(2,1)S(1)}, bf16[16,1280]{1,0:T(8,128)(2,1)S(1)}, u32[]{:S(2)}, u32[]{:S(2)}) collective-permute-start(bf16[16,1280]{1,0:T(8,128)(2,1)S(1)} %fusion.12), channel_id=1, source_target_pairs={{0,6},{1,7},{2,4},{3,5},{4,2},{5,3},{6,0},{7,1},{8,14},{9,15},{10,... | collective-permute-start | bytes 122888 | tf_op jit(solution)/shard_map/ppermute | solution.py:32
  146.7 5.3 %collective-permute-start.40 = (bf16[16,1280]{1,0:T(8,128)(2,1)S(1)}, bf16[16,1280]{1,0:T(8,128)(2,1)S(1)}, u32[]{:S(2)}, u32[]{:S(2)}) collective-permute-start(bf16[16,1280]{1,0:T(8,128)(2,1)S(1)} %add_convert_fusion), channel_id=1, source_target_pairs={{0,9},{1,8},{2,11},{3,10},{4,13},{5,12},{6,15},{7,14},{8,1},{9,0},... | collective-permute-start | bytes 122888 | tf_op jit(solution)/shard_map/ppermute | solution.py:32
  152.2 7.4 %collective-permute-start.16 = (bf16[2,128,256]{2,1,0:T(8,128)(2,1)S(1)}, bf16[2,128,256]{2,1,0:T(8,128)(2,1)S(1)}, u32[]{:S(2)}, u32[]{:S(2)}) collective-permute-start(bf16[2,128,256]{2,1,0:T(8,128)(2,1)S(1)} %get-tuple-element.26), channel_id=1, source_target_pairs={{0,2},{1,3},{2,0},{3,1},{4,6},{5,7},{6,4},{7,5},{8,10},{9,11},{10,... | collective-permute-start | bytes 393224 | tf_op jit(solution)/shard_map/ppermute | solution.py:32
  159.6 6.5 %collective-permute-start.17 = (bf16[128,256]{1,0:T(8,128)(2,1)S(1)}, bf16[128,256]{1,0:T(8,128)(2,1)S(1)}, u32[]{:S(2)}, u32[]{:S(2)}) collective-permute-start(bf16[128,256]{1,0:T(8,128)(2,1)S(1)} %fusion.15), channel_id=1, source_target_pairs={{0,6},{1,7},{2,4},{3,5},{4,2},{5,3},{6,0},{7,1},{8,14},{9,15},{10,... | collective-permute-start | bytes 196616 | tf_op jit(solution)/shard_map/ppermute | solution.py:32
  (26 other events, 210.2 us)
